TPU v7x, 512 devices: a whole 4x4x16 slice. The times are simulated.
512 devices in a mesh: seq: 512 (over x, z, y, core).
Axes of the slice: x: 4, y: 4, z: 16, core: 2. Of those that a mesh axis runs over, the one named last changes fastest.
Arguments:
- signal: bfloat16 [524288, 512], P('seq'), may hold values from -6 to 6
- grad_out: bfloat16 [524288, 512], P('seq'), may hold values from -6 to 6
- conv_weight: bfloat16 [1024, 1024], replicated, may hold values from -0.1875 to 0.1875
- proj_weight: bfloat16 [512, 512], replicated, may hold values from -0.25 to 0.25
Outputs:
- saliency: float32 [524288, 512], P('seq')
All inputs are finite; a program needn't handle non-finite values.
Results may differ from a plain program's by a relative error of at most 0.0013.
Values may be sent and summed in bfloat16 or wider, within the bound.
No kernel may reach another device: no remote copies, remote signals or barrier semaphores. Data moves between devices by JAX's collectives and lax.ppermute only.
A program may use at most 64 MiB of HBM per device.

v0:
```python
import jax
import jax.numpy as jnp
from jax import lax
from jax.sharding import PartitionSpec as P


PARTS = (384, 320)
TWICE = 320


def from_behind(block, axis, distance):
    devices = range(lax.axis_size(axis))
    route = [(i - distance, i) for i in devices if i - distance in devices]
    return lax.ppermute(block, axis, route)


def contract_rows(left, right):
    return lax.dot_general(
        left, right, (((1,), (1,)), ((), ())), preferred_element_type=jnp.float32
    )


def shards(signal, grad_out, conv_weight, proj_weight):
    _, width = signal.shape
    w_past = conv_weight[:width]
    w_now = conv_weight[width:]

    def gradients(past, now, grad):
        own = jnp.dot(now, w_now, preferred_element_type=jnp.float32)
        gates = own + jnp.dot(past, w_past, preferred_element_type=jnp.float32)
        tanh_part = jnp.tanh(gates[:, :width])
        sig_part = jax.nn.sigmoid(gates[:, width:])
        d_mixed = contract_rows(grad, proj_weight)
        d_tanh = d_mixed * sig_part * (1.0 - tanh_part * tanh_part)
        d_sig = d_mixed * tanh_part * sig_part * (1.0 - sig_part)
        return jnp.concatenate([d_tanh, d_sig], 1).astype(jnp.bfloat16)

    def far_of(d_gates):
        return contract_rows(d_gates, w_past).astype(jnp.bfloat16)

    both = jnp.concatenate([signal[:TWICE], grad_out[:TWICE]], 0)
    cuts = [(TWICE + sum(PARTS[:k]), TWICE + sum(PARTS[: k + 1])) for k in range(len(PARTS))]
    past = [from_behind(signal[a:b], "seq", 2) for a, b in cuts]
    ahead = from_behind(both, "seq", -2)
    past_both = from_behind(signal[:TWICE], "seq", 2)
    accs = []
    backs = []
    for k, (a, b) in enumerate(cuts):
        d_gates = gradients(past[k], signal[a:b], grad_out[a:b])
        backs.append(from_behind(far_of(d_gates), "seq", -2))
        acc = grad_out[a:b].astype(jnp.float32) + contract_rows(d_gates, w_now)
        accs.append(lax.optimization_barrier(acc))
    far = far_of(gradients(signal[:TWICE], ahead[:TWICE], ahead[TWICE:]))
    d_gates = gradients(past_both, signal[:TWICE], grad_out[:TWICE])
    first = grad_out[:TWICE].astype(jnp.float32) + contract_rows(d_gates, w_now)
    first = lax.optimization_barrier(first + far.astype(jnp.float32))
    mids = [acc + back.astype(jnp.float32) for acc, back in zip(accs[:-1], backs)]
    out = jnp.concatenate([first, *mids, accs[-1]], 0)
    last = accs[-1] + backs[-1].astype(jnp.float32)
    return lax.dynamic_update_slice(out, last, (cuts[-1][0], 0))


def solution(mesh):
    in_specs = (P("seq", None), P("seq", None), P(), P())
    out_specs = P("seq", None)
    return jax.shard_map(shards, mesh=mesh, in_specs=in_specs, out_specs=out_specs, check_vma=False)
```

profile of v0, /device:TPU:6, one launch (start us, length us, event | category | flops | bytes accessed | tf_op | source)
XLA Modules:
  0.0 57.0 jit_solution(16774672762823596463)
XLA Ops:
  0.0 0.0 copy-start
  0.0 0.0 slice-start
  0.0 1.1 %slice.74 = bf16[384,512]{1,0:T(8,128)(2,1)S(1)} slice(bf16[1024,512]{1,0:T(8,128)(2,1)} %param.4), slice={[320:704], [0:512]} | slice | bytes 786432 | tf_op jit(solution)/shard_map/slice | solution.py:49
  1.1 0.0 copy-start.1
  1.1 0.0 copy-start.2
  1.1 3.7 %collective-permute-start.2 = (bf16[384,512]{1,0:T(8,128)(2,1)S(1)}, bf16[384,512]{1,0:T(8,128)(2,1)S(1)}, u32[]{:S(2)}, u32[]{:S(2)}) collective-permute-start(bf16[384,512]{1,0:T(8,128)(2,1)S(1)} %slice.74), channel_id=1, source_target_pairs={{0,2},{1,3},{2,4},{3,5},{4,6},{5,7},{6,8},{7,9},{8,10},{9,11},{10,... | collective-permute-start | bytes 1179656 | tf_op jit(solution)/shard_map/ppermute | solution.py:14
  4.9 1.1 %fusion.57 = (bf16[320,512]{1,0:T(8,128)(2,1)S(1)}, bf16[320,512]{1,0:T(8,128)(2,1)S(1)}) fusion(bf16[1024,512]{1,0:T(8,128)(2,1)} %param.4), kind=kLoop, calls=%fused_computation.89 | loop fusion | bytes 1310720 | tf_op jit(solution)/shard_map/slice | solution.py:54
  6.0 3.5 %collective-permute-start.4 = (bf16[320,512]{1,0:T(8,128)(2,1)S(1)}, bf16[320,512]{1,0:T(8,128)(2,1)S(1)}, u32[]{:S(2)}, u32[]{:S(2)}) collective-permute-start(bf16[320,512]{1,0:T(8,128)(2,1)S(1)} %get-tuple-element.14), channel_id=1, source_target_pairs={{0,2},{1,3},{2,4},{3,5},{4,6},{5,7},{6,8},{7,9},{8,10},{9,11},{10,... | collective-permute-start | bytes 983048 | tf_op jit(solution)/shard_map/ppermute | solution.py:14
  9.5 3.2 %collective-permute-start = (bf16[320,512]{1,0:T(8,128)(2,1)S(1)}, bf16[320,512]{1,0:T(8,128)(2,1)S(1)}, u32[]{:S(2)}, u32[]{:S(2)}) collective-permute-start(bf16[320,512]{1,0:T(8,128)(2,1)S(1)} %get-tuple-element.13), channel_id=1, source_target_pairs={{0,2},{1,3},{2,4},{3,5},{4,6},{5,7},{6,8},{7,9},{8,10},{9,11},{10,... | collective-permute-start | bytes 983048 | tf_op jit(solution)/shard_map/ppermute | solution.py:14
  12.7 0.0 slice-done
  12.8 9.7 %collective-permute-start.1 = (bf16[640,512]{1,0:T(8,128)(2,1)S(1)}, bf16[640,512]{1,0:T(8,128)(2,1)S(1)}, u32[]{:S(2)}, u32[]{:S(2)}) collective-permute-start(bf16[640,512]{1,0:T(8,128)(2,1)S(1)} %pad_maximum_fusion.2), channel_id=1, source_target_pairs={{2,0},{3,1},{4,2},{5,3},{6,4},{7,5},{8,6},{9,7},{10,8},{11,9},{12,... | collective-permute-start | bytes 1966088 | tf_op jit(solution)/shard_map/ppermute | solution.py:14
  22.5 0.0 copy-done.1
  22.5 0.0 copy-done.2
  22.5 0.5 fusion.30
  23.0 0.5 fusion.34
  23.6 0.5 fusion.41
  24.1 0.6 %fusion.37 = f32[384,1024]{1,0:T(8,128)S(1)} fusion(bf16[1024,1024]{1,0:T(8,128)(2,1)S(1)} %copy-done.1, bf16[1024,512]{1,0:T(8,128)(2,1)S(1)} %copy-done.2), kind=kOutput, calls=%fused_computation.69 | convolution fusion | flops 402653184 | bytes 3014656 | tf_op jit(solution)/shard_map/dot_general | solution.py:29
  24.7 0.0 copy-start.3
  24.7 7.8 %collective-permute-done.4 = bf16[320,512]{1,0:T(8,128)(2,1)S(1)} collective-permute-done((bf16[320,512]{1,0:T(8,128)(2,1)S(1)}, bf16[320,512]{1,0:T(8,128)(2,1)S(1)}, u32[]{:S(2)}, u32[]{:S(2)}) %collective-permute-start.4) | collective-permute-done | bytes 327712 | tf_op jit(solution)/shard_map/ppermute | solution.py:14
  32.5 0.5 convolution_add_fusion.1
  33.0 0.0 copy-done
  33.1 0.0 copy-done.3
  33.1 0.6 %multiply_convert_fusion.3 = (bf16[320,512]{1,0:T(8,128)(2,1)S(1)}, bf16[320,512]{1,0:T(8,128)(2,1)S(1)}) fusion(f32[320,1024]{1,0:T(8,128)S(1)} %convolution_add_fusion.1, bf16[512,512]{1,0:T(8,128)(2,1)S(1)} %copy-done, bf16[1024,512]{1,0:T(8,128)(2,1)S(1)} %copy-done.3), kind=kOutput, calls=%fused_computation.47 | convolution fusion | flops 169902080 | bytes 2818048 | tf_op jit(solution)/shard_map/dot_general | solution.py:18
  33.6 0.6 convolution_add_fusion.5
  34.2 0.5 convolution_convert_fusion.1
  34.8 3.9 %collective-permute-start.5 = (bf16[320,512]{1,0:T(8,128)(2,1)S(1)}, bf16[320,512]{1,0:T(8,128)(2,1)S(1)}, u32[]{:S(2)}, u32[]{:S(2)}) collective-permute-start(bf16[320,512]{1,0:T(8,128)(2,1)S(1)} %convolution_convert_fusion.1), channel_id=1, source_target_pairs={{2,0},{3,1},{4,2},{5,3},{6,4},{7,5},{8,6},{9,7},{10,8},{11,9},{12,... | collective-permute-start | bytes 983048 | tf_op jit(solution)/shard_map/ppermute | solution.py:14
  38.7 0.0 collective-permute-done
  38.7 0.5 convolution_add_fusion.3
  39.2 0.6 %multiply_convert_fusion.7 = (bf16[320,512]{1,0:T(8,128)(2,1)S(1)}, bf16[320,512]{1,0:T(8,128)(2,1)S(1)}) fusion(f32[320,1024]{1,0:T(8,128)S(1)} %convolution_add_fusion.3, bf16[512,512]{1,0:T(8,128)(2,1)S(1)} %copy-done, bf16[1024,512]{1,0:T(8,128)(2,1)S(1)} %copy-done.3), kind=kOutput, calls=%fused_computation.51 | convolution fusion | flops 169902080 | bytes 2818048 | tf_op jit(solution)/shard_map/dot_general | solution.py:18
  39.8 0.0 collective-permute-done.2
  39.8 0.6 %convolution_add_fusion = f32[384,1024]{1,0:T(8,128)S(1)} fusion(f32[384,1024]{1,0:T(8,128)S(1)} %fusion.37, bf16[384,512]{1,0:T(8,128)(2,1)S(1)} %collective-permute-done.2, bf16[1024,1024]{1,0:T(8,128)(2,1)S(1)} %copy-done.1), kind=kOutput, calls=%fused_computation.1 | convolution fusion | flops 403046400 | bytes 4587520 | tf_op jit(solution)/shard_map/dot_general | solution.py:30
  40.4 0.7 %multiply_convert_fusion.1 = (bf16[384,512]{1,0:T(8,128)(2,1)S(1)}, bf16[384,512]{1,0:T(8,128)(2,1)S(1)}) fusion(f32[384,1024]{1,0:T(8,128)S(1)} %convolution_add_fusion, bf16[512,512]{1,0:T(8,128)(2,1)S(1)} %copy-done, bf16[1024,512]{1,0:T(8,128)(2,1)S(1)} %copy-done.3), kind=kOutput, calls=%fused_computation.21 | convolution fusion | flops 203882496 | bytes 3276800 | tf_op jit(solution)/shard_map/dot_general | solution.py:18
  41.1 0.6 %convolution_add_fusion.4 = f32[384,512]{1,0:T(8,128)S(1)} fusion(bf16[384,512]{1,0:T(8,128)(2,1)S(1)} %get-tuple-element.6, bf16[384,512]{1,0:T(8,128)(2,1)S(1)} %get-tuple-element.5, bf16[1024,512]{1,0:T(8,128)(2,1)S(1)} %copy-done.3, bf16[1024,1024]{1,0:T(8,128)(2,1)S(1)} %copy-done.1), kind=kOutput, calls=%fused_computation.5 | convolution fusion | flops 404619264 | bytes 3014656 | tf_op jit(solution)/shard_map/dot_general | solution.py:18
  41.7 0.6 %convolution_convert_fusion = bf16[384,512]{1,0:T(8,128)(2,1)S(1)} fusion(bf16[384,512]{1,0:T(8,128)(2,1)S(1)} %get-tuple-element.6, bf16[384,512]{1,0:T(8,128)(2,1)S(1)} %get-tuple-element.5, bf16[1024,1024]{1,0:T(8,128)(2,1)S(1)} %copy-done.1), kind=kOutput, calls=%fused_computation.9 | convolution fusion | flops 404422656 | bytes 2228224 | tf_op jit(solution)/shard_map/dot_general | solution.py:18
  42.4 3.6 %collective-permute-start.3 = (bf16[384,512]{1,0:T(8,128)(2,1)S(1)}, bf16[384,512]{1,0:T(8,128)(2,1)S(1)}, u32[]{:S(2)}, u32[]{:S(2)}) collective-permute-start(bf16[384,512]{1,0:T(8,128)(2,1)S(1)} %convolution_convert_fusion), channel_id=1, source_target_pairs={{2,0},{3,1},{4,2},{5,3},{6,4},{7,5},{8,6},{9,7},{10,8},{11,9},{12,... | collective-permute-start | bytes 1179656 | tf_op jit(solution)/shard_map/ppermute | solution.py:14
  46.0 0.0 collective-permute-done.1
  46.0 0.5 convolution_add_fusion.2
  46.5 0.6 multiply_convert_fusion.5
  47.1 0.6 fusion.1
  47.7 0.6 %fusion = f32[320,512]{1,0:T(8,128)S(1)} fusion(f32[320,512]{1,0:T(8,128)S(1)} %fusion.1, bf16[320,512]{1,0:T(8,128)(2,1)S(1)} %get-tuple-element.8, bf16[320,512]{1,0:T(8,128)(2,1)S(1)} %get-tuple-element.7, bf16[1024,1024]{1,0:T(8,128)(2,1)S(1)} %copy-done.1, bf16[1024,512]{1,0:T(8,128)(2,1)S(1)} %copy-done.3), kind=kOutput, calls=%fused_computation.8 | convolution fusion | flops 337346560 | bytes 3342336 | tf_op jit(solution)/shard_map/dot_general | solution.py:18
  48.2 6.2 %collective-permute-done.3 = bf16[384,512]{1,0:T(8,128)(2,1)S(1)} collective-permute-done((bf16[384,512]{1,0:T(8,128)(2,1)S(1)}, bf16[384,512]{1,0:T(8,128)(2,1)S(1)}, u32[]{:S(2)}, u32[]{:S(2)}) %collective-permute-start.3) | collective-permute-done | bytes 393248 | tf_op jit(solution)/shard_map/ppermute | solution.py:14
  54.5 0.1 convert_add_fusion
  54.6 1.5 %pad_maximum_fusion = f32[1024,512]{1,0:T(8,128)} fusion(f32[320,512]{1,0:T(8,128)S(1)} %convolution_add_fusion.5, f32[384,512]{1,0:T(8,128)S(1)} %convert_add_fusion, f32[320,512]{1,0:T(8,128)S(1)} %fusion), kind=kLoop, calls=%fused_computation | loop fusion | flops 1048576 | bytes 4194304 | tf_op jit(solution)/shard_map/concatenate | solution.py:58
  56.1 0.0 collective-permute-done.5
  56.1 0.9 %add_dynamic-update-slice_fusion = f32[1024,512]{1,0:T(8,128)} fusion(f32[1024,512]{1,0:T(8,128)} %pad_maximum_fusion, f32[320,512]{1,0:T(8,128)S(1)} %convolution_add_fusion.5, bf16[320,512]{1,0:T(8,128)(2,1)S(1)} %collective-permute-done.5), kind=kLoop, calls=%fused_computation.45 | loop fusion | flops 327680 | bytes 1638400 | tf_op jit(solution)/shard_map/dynamic_update_slice | solution.py:60
  (1 shorter events, 0.0 us)
Async XLA Ops:
  0.0 33.0 %copy-start = (bf16[512,512]{1,0:T(8,128)(2,1)S(1)}, bf16[512,512]{1,0:T(8,128)(2,1)}, u32[]{:S(2)}) copy-start(bf16[512,512]{1,0:T(8,128)(2,1)} %param.7) | copy-start | bytes 1572868
  0.0 12.7 %slice-start = ((bf16[1024,512]{1,0:T(8,128)(2,1)}), bf16[320,512]{1,0:T(8,128)(2,1)S(1)}, s32[]{:S(2)}) async-start(bf16[1024,512]{1,0:T(8,128)(2,1)} %param.5), calls=%async_computation | async-start | bytes 655360 | tf_op jit(solution)/shard_map/slice | solution.py:55
  1.1 21.4 %copy-start.1 = (bf16[1024,1024]{1,0:T(8,128)(2,1)S(1)}, bf16[1024,1024]{1,0:T(8,128)(2,1)}, u32[]{:S(2)}) copy-start(bf16[1024,1024]{1,0:T(8,128)(2,1)} %param.6) | copy-start | bytes 6291460
  1.1 21.4 %copy-start.2 = (bf16[1024,512]{1,0:T(8,128)(2,1)S(1)}, bf16[1024,512]{1,0:T(8,128)(2,1)}, u32[]{:S(2)}) copy-start(bf16[1024,512]{1,0:T(8,128)(2,1)} %param.4) | copy-start | bytes 3145732
  1.1 38.7 %collective-permute-start.2 = (bf16[384,512]{1,0:T(8,128)(2,1)S(1)}, bf16[384,512]{1,0:T(8,128)(2,1)S(1)}, u32[]{:S(2)}, u32[]{:S(2)}) collective-permute-start(bf16[384,512]{1,0:T(8,128)(2,1)S(1)} %slice.74), channel_id=1, source_target_pairs={{0,2},{1,3},{2,4},{3,5},{4,6},{5,7},{6,8},{7,9},{8,10},{9,11},{10,... | collective-permute-start | bytes 1179656 | tf_op jit(solution)/shard_map/ppermute | solution.py:14
  6.0 26.5 %collective-permute-start.4 = (bf16[320,512]{1,0:T(8,128)(2,1)S(1)}, bf16[320,512]{1,0:T(8,128)(2,1)S(1)}, u32[]{:S(2)}, u32[]{:S(2)}) collective-permute-start(bf16[320,512]{1,0:T(8,128)(2,1)S(1)} %get-tuple-element.14), channel_id=1, source_target_pairs={{0,2},{1,3},{2,4},{3,5},{4,6},{5,7},{6,8},{7,9},{8,10},{9,11},{10,... | collective-permute-start | bytes 983048 | tf_op jit(solution)/shard_map/ppermute | solution.py:14
  9.5 29.2 %collective-permute-start = (bf16[320,512]{1,0:T(8,128)(2,1)S(1)}, bf16[320,512]{1,0:T(8,128)(2,1)S(1)}, u32[]{:S(2)}, u32[]{:S(2)}) collective-permute-start(bf16[320,512]{1,0:T(8,128)(2,1)S(1)} %get-tuple-element.13), channel_id=1, source_target_pairs={{0,2},{1,3},{2,4},{3,5},{4,6},{5,7},{6,8},{7,9},{8,10},{9,11},{10,... | collective-permute-start | bytes 983048 | tf_op jit(solution)/shard_map/ppermute | solution.py:14
  12.8 33.2 %collective-permute-start.1 = (bf16[640,512]{1,0:T(8,128)(2,1)S(1)}, bf16[640,512]{1,0:T(8,128)(2,1)S(1)}, u32[]{:S(2)}, u32[]{:S(2)}) collective-permute-start(bf16[640,512]{1,0:T(8,128)(2,1)S(1)} %pad_maximum_fusion.2), channel_id=1, source_target_pairs={{2,0},{3,1},{4,2},{5,3},{6,4},{7,5},{8,6},{9,7},{10,8},{11,9},{12,... | collective-permute-start | bytes 1966088 | tf_op jit(solution)/shard_map/ppermute | solution.py:14
  24.7 8.4 %copy-start.3 = (bf16[1024,512]{1,0:T(8,128)(2,1)S(1)}, bf16[1024,512]{1,0:T(8,128)(2,1)}, u32[]{:S(2)}) copy-start(bf16[1024,512]{1,0:T(8,128)(2,1)} %param.5) | copy-start | bytes 3145732
  34.8 21.3 %collective-permute-start.5 = (bf16[320,512]{1,0:T(8,128)(2,1)S(1)}, bf16[320,512]{1,0:T(8,128)(2,1)S(1)}, u32[]{:S(2)}, u32[]{:S(2)}) collective-permute-start(bf16[320,512]{1,0:T(8,128)(2,1)S(1)} %convolution_convert_fusion.1), channel_id=1, source_target_pairs={{2,0},{3,1},{4,2},{5,3},{6,4},{7,5},{8,6},{9,7},{10,8},{11,9},{12,... | collective-permute-start | bytes 983048 | tf_op jit(solution)/shard_map/ppermute | solution.py:14
  42.4 12.1 %collective-permute-start.3 = (bf16[384,512]{1,0:T(8,128)(2,1)S(1)}, bf16[384,512]{1,0:T(8,128)(2,1)S(1)}, u32[]{:S(2)}, u32[]{:S(2)}) collective-permute-start(bf16[384,512]{1,0:T(8,128)(2,1)S(1)} %convolution_convert_fusion), channel_id=1, source_target_pairs={{2,0},{3,1},{4,2},{5,3},{6,4},{7,5},{8,6},{9,7},{10,8},{11,9},{12,... | collective-permute-start | bytes 1179656 | tf_op jit(solution)/shard_map/ppermute | solution.py:14
where the time goes:
time: 57.3 us; the launch traced here: 57 us
  starting transfers between devices  27.7 us (48%)
  waiting for transfers between devices  14 us (24%)
  matrix products  10.2 us (18%)
  other arithmetic  2.56 us (4%)
  local copies, waits for them, and re-layouts  2.24 us (4%)
    ppermute x6, starting transfers between devices, from_behind(): return lax.ppermute(block, axis, route)  27.7 us
    ppermute x6, waiting for transfers between devices, from_behind(): return lax.ppermute(block, axis, route)  14 us
    dot_general x10, matrix products, contract_rows(): lax.dot_general(left, right, (((1,), (1,)), ((), ())), preferred_element_...  5.84 us
    dot_general x4, matrix products, gradients(): gates = own + jnp.dot(past, w_past, preferred_element_type=jnp.float32)  2.2 us
    dot_general x4, matrix products, gradients(): own = jnp.dot(now, w_now, preferred_element_type=jnp.float32)  2.17 us
    concatenate x1, other arithmetic, shards(): out = jnp.concatenate([first, *mids, accs[-1]], 0)  1.49 us
  transfers between devices with their start and end apart: 6, of which 2 were waited for; matrix products, arithmetic and copies ran while one was open for 23% of the time, Pallas kernels for 0%

commit v1 on v0

--- a/solution.py
+++ b/solution.py
@@ -1,6 +1,10 @@
+import functools
+
 import jax
 import jax.numpy as jnp
 from jax import lax
+from jax.experimental import pallas as pl
+from jax.experimental.pallas import tpu as pltpu
 from jax.sharding import PartitionSpec as P
 
 
@@ -18,6 +22,31 @@
     return lax.dot_general(
         left, right, (((1,), (1,)), ((), ())), preferred_element_type=jnp.float32
     )
+
+
+def cut_body(pieces, *refs):
+    count = len(refs) - 1 - len({o for _, _, o, _, _ in pieces})
+    sources, targets, sems = refs[:count], refs[count:-1], refs[-1]
+    copies = []
+    for k, (source, at, target, to, size) in enumerate(pieces):
+        rows = sources[source].at[pl.ds(at, size)]
+        copies.append(pltpu.make_async_copy(rows, targets[target].at[pl.ds(to, size)], sems.at[k]))
+        copies[-1].start()
+    for copy in copies:
+        copy.wait()
+
+
+def cut_rows(arrays, pieces, sizes, space):
+    width = arrays[0].shape[1]
+    vmem = pl.BlockSpec(memory_space=pltpu.VMEM)
+    return pl.pallas_call(
+        functools.partial(cut_body, pieces),
+        out_shape=[jax.ShapeDtypeStruct((n, width), arrays[0].dtype) for n in sizes],
+        in_specs=[pl.BlockSpec(memory_space=space)] * len(arrays),
+        out_specs=[vmem] * len(sizes),
+        scratch_shapes=[pltpu.SemaphoreType.DMA((len(pieces),))],
+        compiler_params=pltpu.CompilerParams(vmem_limit_bytes=2 * 2**20),
+    )(*arrays)
 
 
 def shards(signal, grad_out, conv_weight, proj_weight):
@@ -38,11 +67,16 @@
     def far_of(d_gates):
         return contract_rows(d_gates, w_past).astype(jnp.bfloat16)
 
-    both = jnp.concatenate([signal[:TWICE], grad_out[:TWICE]], 0)
     cuts = [(TWICE + sum(PARTS[:k]), TWICE + sum(PARTS[: k + 1])) for k in range(len(PARTS))]
-    past = [from_behind(signal[a:b], "seq", 2) for a, b in cuts]
+    pieces = ((0, TWICE, 0, 0, PARTS[0]), (0, 0, 1, 0, TWICE), (1, 0, 1, TWICE, TWICE))
+    held = [pltpu.with_memory_space_constraint(a, pltpu.HBM) for a in (signal, grad_out)]
+    part, both = cut_rows(held, pieces, (PARTS[0], 2 * TWICE), pltpu.HBM)
+    past = [from_behind(part, "seq", 2)]
     ahead = from_behind(both, "seq", -2)
-    past_both = from_behind(signal[:TWICE], "seq", 2)
+    pieces = ((0, cuts[1][0], 0, 0, PARTS[1]), (0, 0, 1, 0, TWICE))
+    part, head = cut_rows([signal, grad_out], pieces, (PARTS[1], TWICE), pltpu.VMEM)
+    past.append(from_behind(part, "seq", 2))
+    past_both = from_behind(head, "seq", 2)
     accs = []
     backs = []
     for k, (a, b) in enumerate(cuts):

time: 57.3 us -> 57.7 us (level)
  Pallas kernels: 0 us -> 1.44 us
  waiting for transfers between devices: 14 us -> 13 us
    unnamed x8 -> x12, local copies, waits for them, and re-layouts: 0.02 us -> 2.53 us
    slice x4 -> x0, local copies, waits for them, and re-layouts: 2.22 us -> none  [the longest x1 1.12 us: shards(): d_gates = gradients(past_both, signal[:TWICE], grad_out[:TWICE])]
    pallas_call x0 -> x2, Pallas kernels: none -> 1.44 us  [cut_rows(): pl.pallas_call(functools.partial(cut_body, pieces), out_shape=[jax.ShapeD...]
    ppermute x6, waiting for transfers between devices: 14 us -> 13 us  [from_behind(): return lax.ppermute(block, axis, route)]
  transfers between devices with their start and end apart: 6 -> 6, of which waited for: 2 -> 3; matrix products, arithmetic and copies ran while one was open for 23% -> 20% of each run, Pallas kernels for 0% -> 2%
where the time goes in v1:
time: 57.7 us; the launch traced here: 57.4 us
  starting transfers between devices  27.6 us (48%)
  waiting for transfers between devices  13 us (23%)
  matrix products  10 us (17%)
  other arithmetic  2.58 us (4%)
  local copies, waits for them, and re-layouts  2.53 us (4%)
  Pallas kernels  1.44 us (2%)
    ppermute x6, starting transfers between devices, from_behind(): return lax.ppermute(block, axis, route)  27.6 us
    ppermute x6, waiting for transfers between devices, from_behind(): return lax.ppermute(block, axis, route)  13 us
    dot_general x10, matrix products, contract_rows(): lax.dot_general(left, right, (((1,), (1,)), ((), ())), preferred_element_...  5.76 us
    unnamed x12, local copies, waits for them, and re-layouts  2.53 us
    dot_general x4, matrix products, gradients(): own = jnp.dot(now, w_now, preferred_element_type=jnp.float32)  2.14 us
    dot_general x4, matrix products, gradients(): gates = own + jnp.dot(past, w_past, preferred_element_type=jnp.float32)  2.11 us
    concatenate x1, other arithmetic, shards(): out = jnp.concatenate([first, *mids, accs[-1]], 0)  1.55 us
    pallas_call x2, Pallas kernels, cut_rows(): pl.pallas_call(functools.partial(cut_body, pieces), out_shape=[jax.ShapeD...  1.44 us
  transfers between devices with their start and end apart: 6, of which 3 were waited for; matrix products, arithmetic and copies ran while one was open for 20% of the time, Pallas kernels for 2%

profile of v1, /device:TPU:6, one launch (start us, length us, event | category | flops | bytes accessed | tf_op | source)
XLA Modules:
  0.0 57.4 jit_solution(11906911554960634089)
XLA Ops:
  0.0 0.0 copy-start
  0.0 0.0 copy-start.1
  0.0 1.3 %copy-done.1 = bf16[1024,512]{1,0:T(8,128)(2,1)S(1)} copy-done((bf16[1024,512]{1,0:T(8,128)(2,1)S(1)}, bf16[1024,512]{1,0:T(8,128)(2,1)}, u32[]{:S(2)}) %copy-start.1) | copy-done | bytes 1048600
  1.3 0.0 copy-start.3
  1.3 1.2 %copy-done.3 = bf16[1024,512]{1,0:T(8,128)(2,1)S(1)} copy-done((bf16[1024,512]{1,0:T(8,128)(2,1)S(1)}, bf16[1024,512]{1,0:T(8,128)(2,1)}, u32[]{:S(2)}) %copy-start.3) | copy-done | bytes 1048600
  2.5 0.0 copy-start.5
  2.5 0.2 shard_map.46
  2.7 0.0 copy-start.2
  2.8 3.6 %collective-permute-start = (bf16[320,512]{1,0:T(8,128)(2,1)S(1)}, bf16[320,512]{1,0:T(8,128)(2,1)S(1)}, u32[]{:S(2)}, u32[]{:S(2)}) collective-permute-start(bf16[320,512]{1,0:T(8,128)(2,1)S(1)} %get-tuple-element.9), channel_id=1, source_target_pairs={{0,2},{1,3},{2,4},{3,5},{4,6},{5,7},{6,8},{7,9},{8,10},{9,11},{10,... | collective-permute-start | bytes 983048 | tf_op jit(solution)/shard_map/ppermute | solution.py:18
  6.4 3.5 %collective-permute-start.4 = (bf16[320,512]{1,0:T(8,128)(2,1)S(1)}, bf16[320,512]{1,0:T(8,128)(2,1)S(1)}, u32[]{:S(2)}, u32[]{:S(2)}) collective-permute-start(bf16[320,512]{1,0:T(8,128)(2,1)S(1)} %get-tuple-element.12), channel_id=1, source_target_pairs={{0,2},{1,3},{2,4},{3,5},{4,6},{5,7},{6,8},{7,9},{8,10},{9,11},{10,... | collective-permute-start | bytes 983048 | tf_op jit(solution)/shard_map/ppermute | solution.py:18
  9.9 1.2 %shard_map.47 = (bf16[384,512]{1,0:T(8,128)(2,1)S(1)}, bf16[640,512]{1,0:T(8,128)(2,1)S(1)}) custom-call(bf16[1024,512]{1,0:T(8,128)(2,1)} %refs_0_.3, bf16[1024,512]{1,0:T(8,128)(2,1)} %refs_1_.3), custom_call_target="tpu_custom_call" | custom-call | tf_op jit(solution)/shard_map/pallas_call | solution.py:42
  11.1 3.2 %collective-permute-start.2 = (bf16[384,512]{1,0:T(8,128)(2,1)S(1)}, bf16[384,512]{1,0:T(8,128)(2,1)S(1)}, u32[]{:S(2)}, u32[]{:S(2)}) collective-permute-start(bf16[384,512]{1,0:T(8,128)(2,1)S(1)} %get-tuple-element.11), channel_id=1, source_target_pairs={{0,2},{1,3},{2,4},{3,5},{4,6},{5,7},{6,8},{7,9},{8,10},{9,11},{10,... | collective-permute-start | bytes 1179656 | tf_op jit(solution)/shard_map/ppermute | solution.py:18
  14.3 9.7 %collective-permute-start.1 = (bf16[640,512]{1,0:T(8,128)(2,1)S(1)}, bf16[640,512]{1,0:T(8,128)(2,1)S(1)}, u32[]{:S(2)}, u32[]{:S(2)}) collective-permute-start(bf16[640,512]{1,0:T(8,128)(2,1)S(1)} %get-tuple-element.10), channel_id=1, source_target_pairs={{2,0},{3,1},{4,2},{5,3},{6,4},{7,5},{8,6},{9,7},{10,8},{11,9},{12,... | collective-permute-start | bytes 1966088 | tf_op jit(solution)/shard_map/ppermute | solution.py:18
  24.0 0.0 copy-done.5
  24.0 0.0 copy-done.2
  24.0 0.5 fusion.34
  24.6 0.5 fusion.43
  25.1 0.5 fusion.27
  25.6 0.6 %fusion.20 = f32[384,1024]{1,0:T(8,128)S(1)} fusion(bf16[1024,512]{1,0:T(8,128)(2,1)S(1)} %copy-done.2, bf16[1024,1024]{1,0:T(8,128)(2,1)S(1)} %copy-done.5), kind=kOutput, calls=%fused_computation.51 | convolution fusion | flops 402653184 | bytes 3014656 | tf_op jit(solution)/shard_map/dot_general | solution.py:58
  26.2 0.0 copy-start.4
  26.2 6.3 %collective-permute-done.4 = bf16[320,512]{1,0:T(8,128)(2,1)S(1)} collective-permute-done((bf16[320,512]{1,0:T(8,128)(2,1)S(1)}, bf16[320,512]{1,0:T(8,128)(2,1)S(1)}, u32[]{:S(2)}, u32[]{:S(2)}) %collective-permute-start.4) | collective-permute-done | bytes 327712 | tf_op jit(solution)/shard_map/ppermute | solution.py:18
  32.6 0.5 convolution_add_fusion.1
  33.1 0.0 copy-done
  33.1 0.0 copy-done.4
  33.1 0.6 multiply_convert_fusion.3
  33.7 0.5 convolution_add_fusion.5
  34.2 0.5 convolution_convert_fusion.1
  34.8 3.9 %collective-permute-start.5 = (bf16[320,512]{1,0:T(8,128)(2,1)S(1)}, bf16[320,512]{1,0:T(8,128)(2,1)S(1)}, u32[]{:S(2)}, u32[]{:S(2)}) collective-permute-start(bf16[320,512]{1,0:T(8,128)(2,1)S(1)} %convolution_convert_fusion.1), channel_id=1, source_target_pairs={{2,0},{3,1},{4,2},{5,3},{6,4},{7,5},{8,6},{9,7},{10,8},{11,9},{12,... | collective-permute-start | bytes 983048 | tf_op jit(solution)/shard_map/ppermute | solution.py:18
  38.7 0.0 collective-permute-done
  38.7 0.5 convolution_add_fusion.3
  39.2 0.6 %multiply_convert_fusion.7 = (bf16[320,512]{1,0:T(8,128)(2,1)S(1)}, bf16[320,512]{1,0:T(8,128)(2,1)S(1)}) fusion(f32[320,1024]{1,0:T(8,128)S(1)} %convolution_add_fusion.3, bf16[512,512]{1,0:T(8,128)(2,1)S(1)} %copy-done, bf16[1024,512]{1,0:T(8,128)(2,1)S(1)} %copy-done.4), kind=kOutput, calls=%fused_computation.50 | convolution fusion | flops 169902080 | bytes 2818048 | tf_op jit(solution)/shard_map/dot_general | solution.py:22
  39.8 0.3 collective-permute-done.2
  40.2 0.6 convolution_add_fusion
  40.7 0.7 %multiply_convert_fusion.1 = (bf16[384,512]{1,0:T(8,128)(2,1)S(1)}, bf16[384,512]{1,0:T(8,128)(2,1)S(1)}) fusion(f32[384,1024]{1,0:T(8,128)S(1)} %convolution_add_fusion, bf16[512,512]{1,0:T(8,128)(2,1)S(1)} %copy-done, bf16[1024,512]{1,0:T(8,128)(2,1)S(1)} %copy-done.4), kind=kOutput, calls=%fused_computation.21 | convolution fusion | flops 203882496 | bytes 3276800 | tf_op jit(solution)/shard_map/dot_general | solution.py:22
  41.4 0.6 %convolution_add_fusion.4 = f32[384,512]{1,0:T(8,128)S(1)} fusion(bf16[384,512]{1,0:T(8,128)(2,1)S(1)} %get-tuple-element.14, bf16[384,512]{1,0:T(8,128)(2,1)S(1)} %get-tuple-element.13, bf16[1024,512]{1,0:T(8,128)(2,1)S(1)} %copy-done.4, bf16[1024,1024]{1,0:T(8,128)(2,1)S(1)} %copy-done.5), kind=kOutput, calls=%fused_computation.5 | convolution fusion | flops 404619264 | bytes 3014656 | tf_op jit(solution)/shard_map/dot_general | solution.py:22
  42.0 0.6 %convolution_convert_fusion = bf16[384,512]{1,0:T(8,128)(2,1)S(1)} fusion(bf16[384,512]{1,0:T(8,128)(2,1)S(1)} %get-tuple-element.14, bf16[384,512]{1,0:T(8,128)(2,1)S(1)} %get-tuple-element.13, bf16[1024,1024]{1,0:T(8,128)(2,1)S(1)} %copy-done.5), kind=kOutput, calls=%fused_computation.9 | convolution fusion | flops 404422656 | bytes 2228224 | tf_op jit(solution)/shard_map/dot_general | solution.py:22
  42.6 3.6 %collective-permute-start.3 = (bf16[384,512]{1,0:T(8,128)(2,1)S(1)}, bf16[384,512]{1,0:T(8,128)(2,1)S(1)}, u32[]{:S(2)}, u32[]{:S(2)}) collective-permute-start(bf16[384,512]{1,0:T(8,128)(2,1)S(1)} %convolution_convert_fusion), channel_id=1, source_target_pairs={{2,0},{3,1},{4,2},{5,3},{6,4},{7,5},{8,6},{9,7},{10,8},{11,9},{12,... | collective-permute-start | bytes 1179656 | tf_op jit(solution)/shard_map/ppermute | solution.py:18
  46.3 0.0 collective-permute-done.1
  46.3 0.5 convolution_add_fusion.2
  46.8 0.6 %multiply_convert_fusion.5 = (bf16[320,512]{1,0:T(8,128)(2,1)S(1)}, bf16[320,512]{1,0:T(8,128)(2,1)S(1)}) fusion(f32[320,1024]{1,0:T(8,128)S(1)} %convolution_add_fusion.2, bf16[512,512]{1,0:T(8,128)(2,1)S(1)} %copy-done, bf16[640,512]{1,0:T(8,128)(2,1)S(1)} %collective-permute-done.1), kind=kOutput, calls=%fused_computation.48 | convolution fusion | flops 169902080 | bytes 2818048 | tf_op jit(solution)/shard_map/dot_general | solution.py:22
  47.4 0.5 fusion.1
  47.9 0.5 fusion
  48.5 6.3 %collective-permute-done.3 = bf16[384,512]{1,0:T(8,128)(2,1)S(1)} collective-permute-done((bf16[384,512]{1,0:T(8,128)(2,1)S(1)}, bf16[384,512]{1,0:T(8,128)(2,1)S(1)}, u32[]{:S(2)}, u32[]{:S(2)}) %collective-permute-start.3) | collective-permute-done | bytes 393248 | tf_op jit(solution)/shard_map/ppermute | solution.py:18
  54.8 0.1 convert_add_fusion
  54.9 1.6 %pad_maximum_fusion = f32[1024,512]{1,0:T(8,128)} fusion(f32[320,512]{1,0:T(8,128)S(1)} %convolution_add_fusion.5, f32[384,512]{1,0:T(8,128)S(1)} %convert_add_fusion, f32[320,512]{1,0:T(8,128)S(1)} %fusion), kind=kLoop, calls=%fused_computation | loop fusion | flops 1048576 | bytes 4194304 | tf_op jit(solution)/shard_map/concatenate | solution.py:92
  56.5 0.0 collective-permute-done.5
  56.5 0.9 %add_dynamic-update-slice_fusion = f32[1024,512]{1,0:T(8,128)} fusion(f32[1024,512]{1,0:T(8,128)} %pad_maximum_fusion, f32[320,512]{1,0:T(8,128)S(1)} %convolution_add_fusion.5, bf16[320,512]{1,0:T(8,128)(2,1)S(1)} %collective-permute-done.5), kind=kLoop, calls=%fused_computation.44 | loop fusion | flops 327680 | bytes 1638400 | tf_op jit(solution)/shard_map/dynamic_update_slice | solution.py:94
Async XLA Ops:
  0.0 33.1 %copy-start = (bf16[512,512]{1,0:T(8,128)(2,1)S(1)}, bf16[512,512]{1,0:T(8,128)(2,1)}, u32[]{:S(2)}) copy-start(bf16[512,512]{1,0:T(8,128)(2,1)} %param.7) | copy-start | bytes 1572868
  0.0 1.3 %copy-start.1 = (bf16[1024,512]{1,0:T(8,128)(2,1)S(1)}, bf16[1024,512]{1,0:T(8,128)(2,1)}, u32[]{:S(2)}) copy-start(bf16[1024,512]{1,0:T(8,128)(2,1)} %refs_0_.3) | copy-start | bytes 3145732
  1.3 1.2 %copy-start.3 = (bf16[1024,512]{1,0:T(8,128)(2,1)S(1)}, bf16[1024,512]{1,0:T(8,128)(2,1)}, u32[]{:S(2)}) copy-start(bf16[1024,512]{1,0:T(8,128)(2,1)} %refs_1_.3) | copy-start | bytes 3145732
  2.5 21.5 %copy-start.5 = (bf16[1024,1024]{1,0:T(8,128)(2,1)S(1)}, bf16[1024,1024]{1,0:T(8,128)(2,1)}, u32[]{:S(2)}) copy-start(bf16[1024,1024]{1,0:T(8,128)(2,1)} %param.6) | copy-start | bytes 6291460
  2.7 21.3 %copy-start.2 = (bf16[1024,512]{1,0:T(8,128)(2,1)S(1)}, bf16[1024,512]{1,0:T(8,128)(2,1)}, u32[]{:S(2)}) copy-start(bf16[1024,512]{1,0:T(8,128)(2,1)} %refs_0_.3) | copy-start | bytes 3145732
  2.8 36.0 %collective-permute-start = (bf16[320,512]{1,0:T(8,128)(2,1)S(1)}, bf16[320,512]{1,0:T(8,128)(2,1)S(1)}, u32[]{:S(2)}, u32[]{:S(2)}) collective-permute-start(bf16[320,512]{1,0:T(8,128)(2,1)S(1)} %get-tuple-element.9), channel_id=1, source_target_pairs={{0,2},{1,3},{2,4},{3,5},{4,6},{5,7},{6,8},{7,9},{8,10},{9,11},{10,... | collective-permute-start | bytes 983048 | tf_op jit(solution)/shard_map/ppermute | solution.py:18
  6.4 26.2 %collective-permute-start.4 = (bf16[320,512]{1,0:T(8,128)(2,1)S(1)}, bf16[320,512]{1,0:T(8,128)(2,1)S(1)}, u32[]{:S(2)}, u32[]{:S(2)}) collective-permute-start(bf16[320,512]{1,0:T(8,128)(2,1)S(1)} %get-tuple-element.12), channel_id=1, source_target_pairs={{0,2},{1,3},{2,4},{3,5},{4,6},{5,7},{6,8},{7,9},{8,10},{9,11},{10,... | collective-permute-start | bytes 983048 | tf_op jit(solution)/shard_map/ppermute | solution.py:18
  11.1 29.1 %collective-permute-start.2 = (bf16[384,512]{1,0:T(8,128)(2,1)S(1)}, bf16[384,512]{1,0:T(8,128)(2,1)S(1)}, u32[]{:S(2)}, u32[]{:S(2)}) collective-permute-start(bf16[384,512]{1,0:T(8,128)(2,1)S(1)} %get-tuple-element.11), channel_id=1, source_target_pairs={{0,2},{1,3},{2,4},{3,5},{4,6},{5,7},{6,8},{7,9},{8,10},{9,11},{10,... | collective-permute-start | bytes 1179656 | tf_op jit(solution)/shard_map/ppermute | solution.py:18
  14.3 32.0 %collective-permute-start.1 = (bf16[640,512]{1,0:T(8,128)(2,1)S(1)}, bf16[640,512]{1,0:T(8,128)(2,1)S(1)}, u32[]{:S(2)}, u32[]{:S(2)}) collective-permute-start(bf16[640,512]{1,0:T(8,128)(2,1)S(1)} %get-tuple-element.10), channel_id=1, source_target_pairs={{2,0},{3,1},{4,2},{5,3},{6,4},{7,5},{8,6},{9,7},{10,8},{11,9},{12,... | collective-permute-start | bytes 1966088 | tf_op jit(solution)/shard_map/ppermute | solution.py:18
  26.2 6.9 %copy-start.4 = (bf16[1024,512]{1,0:T(8,128)(2,1)S(1)}, bf16[1024,512]{1,0:T(8,128)(2,1)}, u32[]{:S(2)}) copy-start(bf16[1024,512]{1,0:T(8,128)(2,1)} %refs_1_.3) | copy-start | bytes 3145732
  34.8 21.7 %collective-permute-start.5 = (bf16[320,512]{1,0:T(8,128)(2,1)S(1)}, bf16[320,512]{1,0:T(8,128)(2,1)S(1)}, u32[]{:S(2)}, u32[]{:S(2)}) collective-permute-start(bf16[320,512]{1,0:T(8,128)(2,1)S(1)} %convolution_convert_fusion.1), channel_id=1, source_target_pairs={{2,0},{3,1},{4,2},{5,3},{6,4},{7,5},{8,6},{9,7},{10,8},{11,9},{12,... | collective-permute-start | bytes 983048 | tf_op jit(solution)/shard_map/ppermute | solution.py:18
  42.6 12.2 %collective-permute-start.3 = (bf16[384,512]{1,0:T(8,128)(2,1)S(1)}, bf16[384,512]{1,0:T(8,128)(2,1)S(1)}, u32[]{:S(2)}, u32[]{:S(2)}) collective-permute-start(bf16[384,512]{1,0:T(8,128)(2,1)S(1)} %convolution_convert_fusion), channel_id=1, source_target_pairs={{2,0},{3,1},{4,2},{5,3},{6,4},{7,5},{8,6},{9,7},{10,8},{11,9},{12,... | collective-permute-start | bytes 1179656 | tf_op jit(solution)/shard_map/ppermute | solution.py:18

commit v2 on v1

--- a/solution.py
+++ b/solution.py
@@ -8,8 +8,8 @@
 from jax.sharding import PartitionSpec as P
 
 
-PARTS = (384, 320)
-TWICE = 320
+PARTS = (352, 320)
+TWICE = 352
 
 
 def from_behind(block, axis, distance):
@@ -47,6 +47,33 @@
         scratch_shapes=[pltpu.SemaphoreType.DMA((len(pieces),))],
         compiler_params=pltpu.CompilerParams(vmem_limit_bytes=2 * 2**20),
     )(*arrays)
+
+
+def last_body(start, whole, acc, back, out, held, sems):
+    count = sems.shape[0]
+    size = acc.shape[0] // count
+    copies = []
+    for k in range(count):
+        r = pl.ds(k * size, size)
+        held[r] = acc[r] + back[r].astype(jnp.float32)
+        copies.append(pltpu.make_async_copy(held.at[r], out.at[pl.ds(start + k * size, size)], sems.at[k]))
+        copies[-1].start()
+    for copy in copies:
+        copy.wait()
+
+
+def put_last(whole, acc, back, start):
+    vmem, anywhere = (pl.BlockSpec(memory_space=m) for m in (pltpu.VMEM, pl.ANY))
+    return pl.pallas_call(
+        functools.partial(last_body, start),
+        out_shape=jax.ShapeDtypeStruct(whole.shape, whole.dtype),
+        in_specs=[anywhere, vmem, vmem],
+        out_specs=anywhere,
+        scratch_shapes=[pltpu.VMEM(acc.shape, acc.dtype), pltpu.SemaphoreType.DMA((4,))],
+        input_output_aliases={0: 0},
+        compiler_params=pltpu.CompilerParams(vmem_limit_bytes=4 * 2**20),
+        name="put_last",
+    )(whole, acc, back)
 
 
 def shards(signal, grad_out, conv_weight, proj_weight):
@@ -90,8 +117,7 @@
     first = lax.optimization_barrier(first + far.astype(jnp.float32))
     mids = [acc + back.astype(jnp.float32) for acc, back in zip(accs[:-1], backs)]
     out = jnp.concatenate([first, *mids, accs[-1]], 0)
-    last = accs[-1] + backs[-1].astype(jnp.float32)
-    return lax.dynamic_update_slice(out, last, (cuts[-1][0], 0))
+    return put_last(out, accs[-1], backs[-1], cuts[-1][0])
 
 
 def solution(mesh):

time: 57.7 us -> 57 us (0.988)
  waiting for transfers between devices: 13 us -> 11.5 us
  other arithmetic: 2.58 us -> 1.58 us
  Pallas kernels: 1.44 us -> 2.37 us
  local copies, waits for them, and re-layouts: 2.53 us -> 3.21 us
    ppermute x6, waiting for transfers between devices: 13 us -> 11.5 us  [from_behind(): return lax.ppermute(block, axis, route)]
    dynamic_update_slice x1 -> x0, other arithmetic: 0.92 us -> none  [shards(): return lax.dynamic_update_slice(out, last, (cuts[-1][0], 0))]
    pallas_call x0 -> x1, Pallas kernels: none -> 0.88 us  [put_last(): pl.pallas_call(functools.partial(last_body, start), out_shape=jax.ShapeDt...]
    unnamed x12, local copies, waits for them, and re-layouts: 2.53 us -> 3.21 us
  transfers between devices with their start and end apart: 6 -> 6, of which waited for: 3 -> 2; matrix products, arithmetic and copies ran while one was open for 20% -> 21% of each run, Pallas kernels for 2% -> 2%
where the time goes in v2:
time: 57 us; the launch traced here: 56.7 us
  starting transfers between devices  27.6 us (48%)
  waiting for transfers between devices  11.5 us (20%)
  matrix products  10.2 us (18%)
  local copies, waits for them, and re-layouts  3.21 us (6%)
  Pallas kernels  2.37 us (4%)
  other arithmetic  1.58 us (3%)
    ppermute x6, starting transfers between devices, from_behind(): return lax.ppermute(block, axis, route)  27.6 us
    ppermute x6, waiting for transfers between devices, from_behind(): return lax.ppermute(block, axis, route)  11.5 us
    dot_general x10, matrix products, contract_rows(): lax.dot_general(left, right, (((1,), (1,)), ((), ())), preferred_element_...  5.83 us
    unnamed x12, local copies, waits for them, and re-layouts  3.21 us
    dot_general x4, matrix products, gradients(): own = jnp.dot(now, w_now, preferred_element_type=jnp.float32)  2.17 us
    dot_general x4, matrix products, gradients(): gates = own + jnp.dot(past, w_past, preferred_element_type=jnp.float32)  2.15 us
    pallas_call x2, Pallas kernels, cut_rows(): pl.pallas_call(functools.partial(cut_body, pieces), out_shape=[jax.ShapeD...  1.49 us
    concatenate x1, other arithmetic, shards(): out = jnp.concatenate([first, *mids, accs[-1]], 0)  1.49 us
  transfers between devices with their start and end apart: 6, of which 2 were waited for; matrix products, arithmetic and copies ran while one was open for 21% of the time, Pallas kernels for 2%

profile of v2, /device:TPU:6, one launch (start us, length us, event | category | flops | bytes accessed | tf_op | source)
XLA Modules:
  0.0 56.7 jit_solution(4975825106487549266)
XLA Ops:
  0.0 0.0 copy-start
  0.0 0.0 copy-start.1
  0.0 1.3 %copy-done.1 = bf16[1024,512]{1,0:T(8,128)(2,1)S(1)} copy-done((bf16[1024,512]{1,0:T(8,128)(2,1)S(1)}, bf16[1024,512]{1,0:T(8,128)(2,1)}, u32[]{:S(2)}) %copy-start.1) | copy-done | bytes 1048600
  1.3 0.0 copy-start.3
  1.3 1.2 %copy-done.3 = bf16[1024,512]{1,0:T(8,128)(2,1)S(1)} copy-done((bf16[1024,512]{1,0:T(8,128)(2,1)S(1)}, bf16[1024,512]{1,0:T(8,128)(2,1)}, u32[]{:S(2)}) %copy-start.3) | copy-done | bytes 1048600
  2.5 0.0 copy-start.5
  2.5 0.3 shard_map.46
  2.8 0.0 copy-start.2
  2.8 3.6 %collective-permute-start.4 = (bf16[320,512]{1,0:T(8,128)(2,1)S(1)}, bf16[320,512]{1,0:T(8,128)(2,1)S(1)}, u32[]{:S(2)}, u32[]{:S(2)}) collective-permute-start(bf16[320,512]{1,0:T(8,128)(2,1)S(1)} %get-tuple-element.12), channel_id=1, source_target_pairs={{0,2},{1,3},{2,4},{3,5},{4,6},{5,7},{6,8},{7,9},{8,10},{9,11},{10,... | collective-permute-start | bytes 983048 | tf_op jit(solution)/shard_map/ppermute | solution.py:18
  6.4 3.5 %collective-permute-start = (bf16[352,512]{1,0:T(8,128)(2,1)S(1)}, bf16[352,512]{1,0:T(8,128)(2,1)S(1)}, u32[]{:S(2)}, u32[]{:S(2)}) collective-permute-start(bf16[352,512]{1,0:T(8,128)(2,1)S(1)} %get-tuple-element.9), channel_id=1, source_target_pairs={{0,2},{1,3},{2,4},{3,5},{4,6},{5,7},{6,8},{7,9},{8,10},{9,11},{10,... | collective-permute-start | bytes 1081352 | tf_op jit(solution)/shard_map/ppermute | solution.py:18
  9.9 1.2 %shard_map.47 = (bf16[352,512]{1,0:T(8,128)(2,1)S(1)}, bf16[704,512]{1,0:T(8,128)(2,1)S(1)}) custom-call(bf16[1024,512]{1,0:T(8,128)(2,1)} %refs_0_.3, bf16[1024,512]{1,0:T(8,128)(2,1)} %refs_1_.3), custom_call_target="tpu_custom_call" | custom-call | tf_op jit(solution)/shard_map/pallas_call | solution.py:42
  11.2 3.2 %collective-permute-start.2 = (bf16[352,512]{1,0:T(8,128)(2,1)S(1)}, bf16[352,512]{1,0:T(8,128)(2,1)S(1)}, u32[]{:S(2)}, u32[]{:S(2)}) collective-permute-start(bf16[352,512]{1,0:T(8,128)(2,1)S(1)} %get-tuple-element.11), channel_id=1, source_target_pairs={{0,2},{1,3},{2,4},{3,5},{4,6},{5,7},{6,8},{7,9},{8,10},{9,11},{10,... | collective-permute-start | bytes 1081352 | tf_op jit(solution)/shard_map/ppermute | solution.py:18
  14.4 9.7 %collective-permute-start.1 = (bf16[704,512]{1,0:T(8,128)(2,1)S(1)}, bf16[704,512]{1,0:T(8,128)(2,1)S(1)}, u32[]{:S(2)}, u32[]{:S(2)}) collective-permute-start(bf16[704,512]{1,0:T(8,128)(2,1)S(1)} %get-tuple-element.10), channel_id=1, source_target_pairs={{2,0},{3,1},{4,2},{5,3},{6,4},{7,5},{8,6},{9,7},{10,8},{11,9},{12,... | collective-permute-start | bytes 2162696 | tf_op jit(solution)/shard_map/ppermute | solution.py:18
  24.1 0.0 copy-done.5
  24.1 0.0 copy-done.2
  24.1 0.6 fusion.29
  24.7 0.6 fusion.31
  25.2 0.5 fusion.25
  25.8 0.6 fusion.23
  26.3 0.0 copy-start.4
  26.3 0.0 collective-permute-done.4
  26.3 0.5 convolution_add_fusion.3
  26.9 0.0 copy-done
  26.9 0.7 %copy-done.4 = bf16[1024,512]{1,0:T(8,128)(2,1)S(1)} copy-done((bf16[1024,512]{1,0:T(8,128)(2,1)S(1)}, bf16[1024,512]{1,0:T(8,128)(2,1)}, u32[]{:S(2)}) %copy-start.4) | copy-done | bytes 1048600
  27.5 0.6 %multiply_convert_fusion.7 = (bf16[320,512]{1,0:T(8,128)(2,1)S(1)}, bf16[320,512]{1,0:T(8,128)(2,1)S(1)}) fusion(f32[320,1024]{1,0:T(8,128)S(1)} %convolution_add_fusion.3, bf16[512,512]{1,0:T(8,128)(2,1)S(1)} %copy-done, bf16[1024,512]{1,0:T(8,128)(2,1)S(1)} %copy-done.4), kind=kOutput, calls=%fused_computation.49 | convolution fusion | flops 169902080 | bytes 2818048 | tf_op jit(solution)/shard_map/dot_general | solution.py:22
  28.1 0.5 convolution_add_fusion.6.acc
  28.7 0.5 convolution_convert_fusion.2
  29.2 3.9 %collective-permute-start.5 = (bf16[320,512]{1,0:T(8,128)(2,1)S(1)}, bf16[320,512]{1,0:T(8,128)(2,1)S(1)}, u32[]{:S(2)}, u32[]{:S(2)}) collective-permute-start(bf16[320,512]{1,0:T(8,128)(2,1)S(1)} %convolution_convert_fusion.2), channel_id=1, source_target_pairs={{2,0},{3,1},{4,2},{5,3},{6,4},{7,5},{8,6},{9,7},{10,8},{11,9},{12,... | collective-permute-start | bytes 983048 | tf_op jit(solution)/shard_map/ppermute | solution.py:18
  33.2 7.0 %collective-permute-done.2 = bf16[352,512]{1,0:T(8,128)(2,1)S(1)} collective-permute-done((bf16[352,512]{1,0:T(8,128)(2,1)S(1)}, bf16[352,512]{1,0:T(8,128)(2,1)S(1)}, u32[]{:S(2)}, u32[]{:S(2)}) %collective-permute-start.2) | collective-permute-done | bytes 360480 | tf_op jit(solution)/shard_map/ppermute | solution.py:18
  40.2 0.5 convolution_add_fusion
  40.7 0.6 %multiply_convert_fusion.1 = (bf16[352,512]{1,0:T(8,128)(2,1)S(1)}, bf16[352,512]{1,0:T(8,128)(2,1)S(1)}) fusion(f32[352,1024]{1,0:T(8,128)S(1)} %convolution_add_fusion, bf16[512,512]{1,0:T(8,128)(2,1)S(1)} %copy-done, bf16[1024,512]{1,0:T(8,128)(2,1)S(1)} %copy-done.4), kind=kOutput, calls=%fused_computation.37 | convolution fusion | flops 186892288 | bytes 3047424 | tf_op jit(solution)/shard_map/dot_general | solution.py:22
  41.4 0.6 %convolution_add_fusion.4 = f32[352,512]{1,0:T(8,128)S(1)} fusion(bf16[352,512]{1,0:T(8,128)(2,1)S(1)} %get-tuple-element.18, bf16[352,512]{1,0:T(8,128)(2,1)S(1)} %get-tuple-element.17, bf16[1024,512]{1,0:T(8,128)(2,1)S(1)} %copy-done.4, bf16[1024,1024]{1,0:T(8,128)(2,1)S(1)} %copy-done.5), kind=kOutput, calls=%fused_computation.5 | convolution fusion | flops 370900992 | bytes 2850816 | tf_op jit(solution)/shard_map/dot_general | solution.py:22
  42.0 0.6 %convolution_convert_fusion = bf16[352,512]{1,0:T(8,128)(2,1)S(1)} fusion(bf16[352,512]{1,0:T(8,128)(2,1)S(1)} %get-tuple-element.18, bf16[352,512]{1,0:T(8,128)(2,1)S(1)} %get-tuple-element.17, bf16[1024,1024]{1,0:T(8,128)(2,1)S(1)} %copy-done.5), kind=kOutput, calls=%fused_computation.9 | convolution fusion | flops 370720768 | bytes 2129920 | tf_op jit(solution)/shard_map/dot_general | solution.py:22
  42.6 3.6 %collective-permute-start.3 = (bf16[352,512]{1,0:T(8,128)(2,1)S(1)}, bf16[352,512]{1,0:T(8,128)(2,1)S(1)}, u32[]{:S(2)}, u32[]{:S(2)}) collective-permute-start(bf16[352,512]{1,0:T(8,128)(2,1)S(1)} %convolution_convert_fusion), channel_id=1, source_target_pairs={{2,0},{3,1},{4,2},{5,3},{6,4},{7,5},{8,6},{9,7},{10,8},{11,9},{12,... | collective-permute-start | bytes 1081352 | tf_op jit(solution)/shard_map/ppermute | solution.py:18
  46.2 0.0 collective-permute-done
  46.2 0.5 convolution_add_fusion.2
  46.8 0.6 %multiply_convert_fusion.5 = (bf16[352,512]{1,0:T(8,128)(2,1)S(1)}, bf16[352,512]{1,0:T(8,128)(2,1)S(1)}) fusion(f32[352,1024]{1,0:T(8,128)S(1)} %convolution_add_fusion.2, bf16[512,512]{1,0:T(8,128)(2,1)S(1)} %copy-done, bf16[1024,512]{1,0:T(8,128)(2,1)S(1)} %copy-done.4), kind=kOutput, calls=%fused_computation.41 | convolution fusion | flops 186892288 | bytes 3047424 | tf_op jit(solution)/shard_map/dot_general | solution.py:22
  47.4 0.0 collective-permute-done.1
  47.4 0.5 convolution_add_fusion.1
  47.9 0.6 %multiply_convert_fusion.3 = (bf16[352,512]{1,0:T(8,128)(2,1)S(1)}, bf16[352,512]{1,0:T(8,128)(2,1)S(1)}) fusion(f32[352,1024]{1,0:T(8,128)S(1)} %convolution_add_fusion.1, bf16[512,512]{1,0:T(8,128)(2,1)S(1)} %copy-done, bf16[704,512]{1,0:T(8,128)(2,1)S(1)} %collective-permute-done.1), kind=kOutput, calls=%fused_computation.39 | convolution fusion | flops 186892288 | bytes 3047424 | tf_op jit(solution)/shard_map/dot_general | solution.py:22
  48.6 0.6 %fusion.1 = f32[352,512]{1,0:T(8,128)S(1)} fusion(bf16[352,512]{1,0:T(8,128)(2,1)S(1)} %get-tuple-element.16, bf16[352,512]{1,0:T(8,128)(2,1)S(1)} %get-tuple-element.15, bf16[1024,1024]{1,0:T(8,128)(2,1)S(1)} %copy-done.5), kind=kOutput, calls=%fused_computation.11 | convolution fusion | flops 370900992 | bytes 2490368 | tf_op jit(solution)/shard_map/dot_general | solution.py:22
  49.1 0.6 %fusion = f32[352,512]{1,0:T(8,128)S(1)} fusion(f32[352,512]{1,0:T(8,128)S(1)} %fusion.1, bf16[352,512]{1,0:T(8,128)(2,1)S(1)} %get-tuple-element.14, bf16[352,512]{1,0:T(8,128)(2,1)S(1)} %get-tuple-element.13, bf16[1024,512]{1,0:T(8,128)(2,1)S(1)} %copy-done.4, bf16[1024,1024]{1,0:T(8,128)(2,1)S(1)} %copy-done.5), kind=kOutput, calls=%fused_computation.7 | convolution fusion | flops 371081216 | bytes 3571712 | tf_op jit(solution)/shard_map/dot_general | solution.py:22
  49.7 4.5 %collective-permute-done.3 = bf16[352,512]{1,0:T(8,128)(2,1)S(1)} collective-permute-done((bf16[352,512]{1,0:T(8,128)(2,1)S(1)}, bf16[352,512]{1,0:T(8,128)(2,1)S(1)}, u32[]{:S(2)}, u32[]{:S(2)}) %collective-permute-start.3) | collective-permute-done | bytes 360480 | tf_op jit(solution)/shard_map/ppermute | solution.py:18
  54.2 0.1 convert_add_fusion
  54.3 1.5 %pad_maximum_fusion.whole = f32[1024,512]{1,0:T(8,128)} fusion(f32[320,512]{1,0:T(8,128)S(1)} %convolution_add_fusion.6.acc, f32[352,512]{1,0:T(8,128)S(1)} %convert_add_fusion, f32[352,512]{1,0:T(8,128)S(1)} %fusion), kind=kLoop, calls=%fused_computation | loop fusion | flops 1048576 | bytes 4194304 | tf_op jit(solution)/shard_map/concatenate | solution.py:119
  55.8 0.0 collective-permute-done.5.back
  55.8 0.9 %put_last.1 = f32[1024,512]{1,0:T(8,128)} custom-call(f32[1024,512]{1,0:T(8,128)} %pad_maximum_fusion.whole, f32[320,512]{1,0:T(8,128)S(1)} %convolution_add_fusion.6.acc, bf16[320,512]{1,0:T(8,128)(2,1)S(1)} %collective-permute-done.5.back), custom_call_target="tpu_custom_call", output_to_operand_aliasing={{}: (0, {})} | custom-call | tf_op jit(solution)/shard_map/put_last/pallas_call | solution.py:67
Async XLA Ops:
  0.0 26.9 %copy-start = (bf16[512,512]{1,0:T(8,128)(2,1)S(1)}, bf16[512,512]{1,0:T(8,128)(2,1)}, u32[]{:S(2)}) copy-start(bf16[512,512]{1,0:T(8,128)(2,1)} %param.7) | copy-start | bytes 1572868
  0.0 1.3 %copy-start.1 = (bf16[1024,512]{1,0:T(8,128)(2,1)S(1)}, bf16[1024,512]{1,0:T(8,128)(2,1)}, u32[]{:S(2)}) copy-start(bf16[1024,512]{1,0:T(8,128)(2,1)} %refs_0_.3) | copy-start | bytes 3145732
  1.3 1.2 %copy-start.3 = (bf16[1024,512]{1,0:T(8,128)(2,1)S(1)}, bf16[1024,512]{1,0:T(8,128)(2,1)}, u32[]{:S(2)}) copy-start(bf16[1024,512]{1,0:T(8,128)(2,1)} %refs_1_.3) | copy-start | bytes 3145732
  2.5 21.6 %copy-start.5 = (bf16[1024,1024]{1,0:T(8,128)(2,1)S(1)}, bf16[1024,1024]{1,0:T(8,128)(2,1)}, u32[]{:S(2)}) copy-start(bf16[1024,1024]{1,0:T(8,128)(2,1)} %param.6) | copy-start | bytes 6291460
  2.8 21.3 %copy-start.2 = (bf16[1024,512]{1,0:T(8,128)(2,1)S(1)}, bf16[1024,512]{1,0:T(8,128)(2,1)}, u32[]{:S(2)}) copy-start(bf16[1024,512]{1,0:T(8,128)(2,1)} %refs_0_.3) | copy-start | bytes 3145732
  2.8 23.5 %collective-permute-start.4 = (bf16[320,512]{1,0:T(8,128)(2,1)S(1)}, bf16[320,512]{1,0:T(8,128)(2,1)S(1)}, u32[]{:S(2)}, u32[]{:S(2)}) collective-permute-start(bf16[320,512]{1,0:T(8,128)(2,1)S(1)} %get-tuple-element.12), channel_id=1, source_target_pairs={{0,2},{1,3},{2,4},{3,5},{4,6},{5,7},{6,8},{7,9},{8,10},{9,11},{10,... | collective-permute-start | bytes 983048 | tf_op jit(solution)/shard_map/ppermute | solution.py:18
  6.4 39.8 %collective-permute-start = (bf16[352,512]{1,0:T(8,128)(2,1)S(1)}, bf16[352,512]{1,0:T(8,128)(2,1)S(1)}, u32[]{:S(2)}, u32[]{:S(2)}) collective-permute-start(bf16[352,512]{1,0:T(8,128)(2,1)S(1)} %get-tuple-element.9), channel_id=1, source_target_pairs={{0,2},{1,3},{2,4},{3,5},{4,6},{5,7},{6,8},{7,9},{8,10},{9,11},{10,... | collective-permute-start | bytes 1081352 | tf_op jit(solution)/shard_map/ppermute | solution.py:18
  11.2 29.0 %collective-permute-start.2 = (bf16[352,512]{1,0:T(8,128)(2,1)S(1)}, bf16[352,512]{1,0:T(8,128)(2,1)S(1)}, u32[]{:S(2)}, u32[]{:S(2)}) collective-permute-start(bf16[352,512]{1,0:T(8,128)(2,1)S(1)} %get-tuple-element.11), channel_id=1, source_target_pairs={{0,2},{1,3},{2,4},{3,5},{4,6},{5,7},{6,8},{7,9},{8,10},{9,11},{10,... | collective-permute-start | bytes 1081352 | tf_op jit(solution)/shard_map/ppermute | solution.py:18
  14.4 33.0 %collective-permute-start.1 = (bf16[704,512]{1,0:T(8,128)(2,1)S(1)}, bf16[704,512]{1,0:T(8,128)(2,1)S(1)}, u32[]{:S(2)}, u32[]{:S(2)}) collective-permute-start(bf16[704,512]{1,0:T(8,128)(2,1)S(1)} %get-tuple-element.10), channel_id=1, source_target_pairs={{2,0},{3,1},{4,2},{5,3},{6,4},{7,5},{8,6},{9,7},{10,8},{11,9},{12,... | collective-permute-start | bytes 2162696 | tf_op jit(solution)/shard_map/ppermute | solution.py:18
  26.3 1.2 %copy-start.4 = (bf16[1024,512]{1,0:T(8,128)(2,1)S(1)}, bf16[1024,512]{1,0:T(8,128)(2,1)}, u32[]{:S(2)}) copy-start(bf16[1024,512]{1,0:T(8,128)(2,1)} %refs_1_.3) | copy-start | bytes 3145732
  29.2 26.6 %collective-permute-start.5 = (bf16[320,512]{1,0:T(8,128)(2,1)S(1)}, bf16[320,512]{1,0:T(8,128)(2,1)S(1)}, u32[]{:S(2)}, u32[]{:S(2)}) collective-permute-start(bf16[320,512]{1,0:T(8,128)(2,1)S(1)} %convolution_convert_fusion.2), channel_id=1, source_target_pairs={{2,0},{3,1},{4,2},{5,3},{6,4},{7,5},{8,6},{9,7},{10,8},{11,9},{12,... | collective-permute-start | bytes 983048 | tf_op jit(solution)/shard_map/ppermute | solution.py:18
  42.6 11.6 %collective-permute-start.3 = (bf16[352,512]{1,0:T(8,128)(2,1)S(1)}, bf16[352,512]{1,0:T(8,128)(2,1)S(1)}, u32[]{:S(2)}, u32[]{:S(2)}) collective-permute-start(bf16[352,512]{1,0:T(8,128)(2,1)S(1)} %convolution_convert_fusion), channel_id=1, source_target_pairs={{2,0},{3,1},{4,2},{5,3},{6,4},{7,5},{8,6},{9,7},{10,8},{11,9},{12,... | collective-permute-start | bytes 1081352 | tf_op jit(solution)/shard_map/ppermute | solution.py:18

commit v3 on v1

--- a/solution.py
+++ b/solution.py
@@ -8,8 +8,9 @@
 from jax.sharding import PartitionSpec as P
 
 
-PARTS = (384, 320)
-TWICE = 320
+PARTS = (416, 256)
+TWICE = 352
+COVER = 10**10
 
 
 def from_behind(block, axis, distance):
@@ -36,7 +37,7 @@
         copy.wait()
 
 
-def cut_rows(arrays, pieces, sizes, space):
+def cut_rows(arrays, pieces, sizes, space, flops):
     width = arrays[0].shape[1]
     vmem = pl.BlockSpec(memory_space=pltpu.VMEM)
     return pl.pallas_call(
@@ -45,6 +46,7 @@
         in_specs=[pl.BlockSpec(memory_space=space)] * len(arrays),
         out_specs=[vmem] * len(sizes),
         scratch_shapes=[pltpu.SemaphoreType.DMA((len(pieces),))],
+        cost_estimate=pl.CostEstimate(flops=flops, bytes_accessed=0, transcendentals=0),
         compiler_params=pltpu.CompilerParams(vmem_limit_bytes=2 * 2**20),
     )(*arrays)
 
@@ -69,23 +71,25 @@
 
     cuts = [(TWICE + sum(PARTS[:k]), TWICE + sum(PARTS[: k + 1])) for k in range(len(PARTS))]
     pieces = ((0, TWICE, 0, 0, PARTS[0]), (0, 0, 1, 0, TWICE), (1, 0, 1, TWICE, TWICE))
+    pieces += ((0, cuts[1][0], 2, 0, PARTS[1]),)
     held = [pltpu.with_memory_space_constraint(a, pltpu.HBM) for a in (signal, grad_out)]
-    part, both = cut_rows(held, pieces, (PARTS[0], 2 * TWICE), pltpu.HBM)
-    past = [from_behind(part, "seq", 2)]
+    sizes = (PARTS[0], 2 * TWICE, PARTS[1])
+    first_part, both, second_part = cut_rows(held, pieces, sizes, pltpu.HBM, 0)
+    parts = (first_part, second_part)
+    past = [from_behind(parts[0], "seq", 2)]
     ahead = from_behind(both, "seq", -2)
-    pieces = ((0, cuts[1][0], 0, 0, PARTS[1]), (0, 0, 1, 0, TWICE))
-    part, head = cut_rows([signal, grad_out], pieces, (PARTS[1], TWICE), pltpu.VMEM)
-    past.append(from_behind(part, "seq", 2))
+    (head,) = cut_rows([both], ((0, 0, 0, 0, TWICE),), (TWICE,), pltpu.VMEM, COVER)
+    past.append(from_behind(parts[1], "seq", 2))
     past_both = from_behind(head, "seq", 2)
     accs = []
     backs = []
     for k, (a, b) in enumerate(cuts):
-        d_gates = gradients(past[k], signal[a:b], grad_out[a:b])
+        d_gates = gradients(past[k], parts[k], grad_out[a:b])
         backs.append(from_behind(far_of(d_gates), "seq", -2))
         acc = grad_out[a:b].astype(jnp.float32) + contract_rows(d_gates, w_now)
         accs.append(lax.optimization_barrier(acc))
-    far = far_of(gradients(signal[:TWICE], ahead[:TWICE], ahead[TWICE:]))
-    d_gates = gradients(past_both, signal[:TWICE], grad_out[:TWICE])
+    far = far_of(gradients(both[:TWICE], ahead[:TWICE], ahead[TWICE:]))
+    d_gates = gradients(past_both, both[:TWICE], both[TWICE:])
     first = grad_out[:TWICE].astype(jnp.float32) + contract_rows(d_gates, w_now)
     first = lax.optimization_barrier(first + far.astype(jnp.float32))
     mids = [acc + back.astype(jnp.float32) for acc, back in zip(accs[:-1], backs)]

time: 57.7 us -> 69.2 us (1.20)
  waiting for transfers between devices: 13 us -> 30.6 us
  starting transfers between devices: 27.6 us -> 23.9 us
  local copies, waits for them, and re-layouts: 2.53 us -> 0.02 us
    ppermute x6, waiting for transfers between devices: 13 us -> 30.6 us  [from_behind(): return lax.ppermute(block, axis, route)]
    ppermute x6, starting transfers between devices: 27.6 us -> 23.9 us  [from_behind(): return lax.ppermute(block, axis, route)]
    unnamed x12 -> x6, local copies, waits for them, and re-layouts: 2.53 us -> 0.02 us
  transfers between devices with their start and end apart: 6 -> 6, of which waited for: 3 -> 2; matrix products, arithmetic and copies ran while one was open for 20% -> 17% of each run, Pallas kernels for 2% -> 0%
where the time goes in v3:
time: 69.2 us; the launch traced here: 69 us
  waiting for transfers between devices  30.6 us (44%)
  starting transfers between devices  23.9 us (35%)
  matrix products  10.2 us (15%)
  other arithmetic  2.48 us (4%)
  Pallas kernels  1.54 us (2%)
    ppermute x6, waiting for transfers between devices, from_behind(): return lax.ppermute(block, axis, route)  30.6 us
    ppermute x6, starting transfers between devices, from_behind(): return lax.ppermute(block, axis, route)  23.9 us
    dot_general x10, matrix products, contract_rows(): lax.dot_general(left, right, (((1,), (1,)), ((), ())), preferred_element_...  5.82 us
    dot_general x4, matrix products, gradients(): gates = own + jnp.dot(past, w_past, preferred_element_type=jnp.float32)  2.18 us
    dot_general x4, matrix products, gradients(): own = jnp.dot(now, w_now, preferred_element_type=jnp.float32)  2.15 us
    pallas_call x2, Pallas kernels, cut_rows(): pl.pallas_call(functools.partial(cut_body, pieces), out_shape=[jax.ShapeD...  1.54 us
    concatenate x1, other arithmetic, shards(): out = jnp.concatenate([first, *mids, accs[-1]], 0)  1.49 us
  transfers between devices with their start and end apart: 6, of which 2 were waited for; matrix products, arithmetic and copies ran while one was open for 17% of the time, Pallas kernels for 0%

profile of v3, /device:TPU:6, one launch (start us, length us, event | category | flops | bytes accessed | tf_op | source)
XLA Modules:
  0.0 69.0 jit_solution(11477537463267189656)
XLA Ops:
  0.0 0.0 copy-start
  0.0 1.4 %shard_map.46 = (bf16[416,512]{1,0:T(8,128)(2,1)S(1)}, bf16[704,512]{1,0:T(8,128)(2,1)S(1)}, bf16[256,512]{1,0:T(8,128)(2,1)S(1)}) custom-call(bf16[1024,512]{1,0:T(8,128)(2,1)} %refs_0_.1, bf16[1024,512]{1,0:T(8,128)(2,1)} %refs_1_.1), custom_call_target="tpu_custom_call" | custom-call | tf_op jit(solution)/shard_map/pallas_call | solution.py:43
  1.4 0.0 copy-start.1
  1.4 14.2 %collective-permute-start.1 = (bf16[704,512]{1,0:T(8,128)(2,1)S(1)}, bf16[704,512]{1,0:T(8,128)(2,1)S(1)}, u32[]{:S(2)}, u32[]{:S(2)}) collective-permute-start(bf16[704,512]{1,0:T(8,128)(2,1)S(1)} %get-tuple-element.8.refs_0_), channel_id=1, source_target_pairs={{2,0},{3,1},{4,2},{5,3},{6,4},{7,5},{8,6},{9,7},{10,8},{11,9},{12,... | collective-permute-start | bytes 2162696 | tf_op jit(solution)/shard_map/ppermute | solution.py:19
  15.7 0.2 shard_map.47
  15.8 1.9 %collective-permute-start = (bf16[352,512]{1,0:T(8,128)(2,1)S(1)}, bf16[352,512]{1,0:T(8,128)(2,1)S(1)}, u32[]{:S(2)}, u32[]{:S(2)}) collective-permute-start(bf16[352,512]{1,0:T(8,128)(2,1)S(1)} %shard_map.47), channel_id=1, source_target_pairs={{0,2},{1,3},{2,4},{3,5},{4,6},{5,7},{6,8},{7,9},{8,10},{9,11},{10,... | collective-permute-start | bytes 1081352 | tf_op jit(solution)/shard_map/ppermute | solution.py:19
  17.8 1.9 %collective-permute-start.2 = (bf16[416,512]{1,0:T(8,128)(2,1)S(1)}, bf16[416,512]{1,0:T(8,128)(2,1)S(1)}, u32[]{:S(2)}, u32[]{:S(2)}) collective-permute-start(bf16[416,512]{1,0:T(8,128)(2,1)S(1)} %get-tuple-element.9), channel_id=1, source_target_pairs={{0,2},{1,3},{2,4},{3,5},{4,6},{5,7},{6,8},{7,9},{8,10},{9,11},{10,... | collective-permute-start | bytes 1277960 | tf_op jit(solution)/shard_map/ppermute | solution.py:19
  19.7 1.9 %collective-permute-start.4 = (bf16[256,512]{1,0:T(8,128)(2,1)S(1)}, bf16[256,512]{1,0:T(8,128)(2,1)S(1)}, u32[]{:S(2)}, u32[]{:S(2)}) collective-permute-start(bf16[256,512]{1,0:T(8,128)(2,1)S(1)} %get-tuple-element.10), channel_id=1, source_target_pairs={{0,2},{1,3},{2,4},{3,5},{4,6},{5,7},{6,8},{7,9},{8,10},{9,11},{10,... | collective-permute-start | bytes 786440 | tf_op jit(solution)/shard_map/ppermute | solution.py:19
  21.6 0.0 copy-done.1
  21.6 0.5 fusion.27
  22.2 0.5 fusion.29
  22.7 0.6 fusion.42
  23.3 0.5 fusion.39
  23.8 0.0 copy-start.2
  23.8 22.7 %collective-permute-done.4 = bf16[256,512]{1,0:T(8,128)(2,1)S(1)} collective-permute-done((bf16[256,512]{1,0:T(8,128)(2,1)S(1)}, bf16[256,512]{1,0:T(8,128)(2,1)S(1)}, u32[]{:S(2)}, u32[]{:S(2)}) %collective-permute-start.4) | collective-permute-done | bytes 262176 | tf_op jit(solution)/shard_map/ppermute | solution.py:19
  46.6 0.5 convolution_add_fusion.3
  47.0 0.0 copy-done
  47.0 0.0 copy-done.2
  47.0 0.5 multiply_convert_fusion.7
  47.6 0.5 convolution_add_fusion.6
  48.0 0.5 convolution_convert_fusion.2
  48.5 1.9 %collective-permute-start.5 = (bf16[256,512]{1,0:T(8,128)(2,1)S(1)}, bf16[256,512]{1,0:T(8,128)(2,1)S(1)}, u32[]{:S(2)}, u32[]{:S(2)}) collective-permute-start(bf16[256,512]{1,0:T(8,128)(2,1)S(1)} %convolution_convert_fusion.2), channel_id=1, source_target_pairs={{2,0},{3,1},{4,2},{5,3},{6,4},{7,5},{8,6},{9,7},{10,8},{11,9},{12,... | collective-permute-start | bytes 786440 | tf_op jit(solution)/shard_map/ppermute | solution.py:19
  50.5 0.0 collective-permute-done
  50.5 0.5 convolution_add_fusion.2
  51.0 0.6 multiply_convert_fusion.5
  51.6 0.0 collective-permute-done.2
  51.7 0.7 convolution_add_fusion
  52.3 0.7 %multiply_convert_fusion.1 = (bf16[416,512]{1,0:T(8,128)(2,1)S(1)}, bf16[416,512]{1,0:T(8,128)(2,1)S(1)}) fusion(f32[416,1024]{1,0:T(8,128)S(1)} %convolution_add_fusion, bf16[512,512]{1,0:T(8,128)(2,1)S(1)} %copy-done, bf16[1024,512]{1,0:T(8,128)(2,1)S(1)} %copy-done.2), kind=kOutput, calls=%fused_computation.21 | convolution fusion | flops 220872704 | bytes 3506176 | tf_op jit(solution)/shard_map/dot_general | solution.py:23
  53.0 0.6 convolution_convert_fusion
  53.7 1.9 %collective-permute-start.3 = (bf16[416,512]{1,0:T(8,128)(2,1)S(1)}, bf16[416,512]{1,0:T(8,128)(2,1)S(1)}, u32[]{:S(2)}, u32[]{:S(2)}) collective-permute-start(bf16[416,512]{1,0:T(8,128)(2,1)S(1)} %convolution_convert_fusion), channel_id=1, source_target_pairs={{2,0},{3,1},{4,2},{5,3},{6,4},{7,5},{8,6},{9,7},{10,8},{11,9},{12,... | collective-permute-start | bytes 1277960 | tf_op jit(solution)/shard_map/ppermute | solution.py:19
  55.6 0.6 convolution_add_fusion.4
  56.2 0.0 collective-permute-done.1
  56.3 0.5 convolution_add_fusion.1
  56.8 0.6 multiply_convert_fusion.3
  57.4 0.6 fusion.1
  58.0 0.6 fusion
  58.6 7.9 %collective-permute-done.3 = bf16[416,512]{1,0:T(8,128)(2,1)S(1)} collective-permute-done((bf16[416,512]{1,0:T(8,128)(2,1)S(1)}, bf16[416,512]{1,0:T(8,128)(2,1)S(1)}, u32[]{:S(2)}, u32[]{:S(2)}) %collective-permute-start.3) | collective-permute-done | bytes 426016 | tf_op jit(solution)/shard_map/ppermute | solution.py:19
  66.5 0.1 convert_add_fusion
  66.6 1.5 %pad_maximum_fusion = f32[1024,512]{1,0:T(8,128)} fusion(f32[256,512]{1,0:T(8,128)S(1)} %convolution_add_fusion.6, f32[416,512]{1,0:T(8,128)S(1)} %convert_add_fusion, f32[352,512]{1,0:T(8,128)S(1)} %fusion), kind=kLoop, calls=%fused_computation | loop fusion | flops 1048576 | bytes 4194304 | tf_op jit(solution)/shard_map/concatenate | solution.py:96
  68.1 0.0 collective-permute-done.5
  68.1 0.9 %add_dynamic-update-slice_fusion = f32[1024,512]{1,0:T(8,128)} fusion(f32[1024,512]{1,0:T(8,128)} %pad_maximum_fusion, f32[256,512]{1,0:T(8,128)S(1)} %convolution_add_fusion.6, bf16[256,512]{1,0:T(8,128)(2,1)S(1)} %collective-permute-done.5), kind=kLoop, calls=%fused_computation.48 | loop fusion | flops 262144 | bytes 1310720 | tf_op jit(solution)/shard_map/dynamic_update_slice | solution.py:98
Async XLA Ops:
  0.0 47.0 %copy-start = (bf16[512,512]{1,0:T(8,128)(2,1)S(1)}, bf16[512,512]{1,0:T(8,128)(2,1)}, u32[]{:S(2)}) copy-start(bf16[512,512]{1,0:T(8,128)(2,1)} %param.7) | copy-start | bytes 1572868
  1.4 20.2 %copy-start.1 = (bf16[1024,1024]{1,0:T(8,128)(2,1)S(1)}, bf16[1024,1024]{1,0:T(8,128)(2,1)}, u32[]{:S(2)}) copy-start(bf16[1024,1024]{1,0:T(8,128)(2,1)} %param.6) | copy-start | bytes 6291460
  1.4 54.8 %collective-permute-start.1 = (bf16[704,512]{1,0:T(8,128)(2,1)S(1)}, bf16[704,512]{1,0:T(8,128)(2,1)S(1)}, u32[]{:S(2)}, u32[]{:S(2)}) collective-permute-start(bf16[704,512]{1,0:T(8,128)(2,1)S(1)} %get-tuple-element.8.refs_0_), channel_id=1, source_target_pairs={{2,0},{3,1},{4,2},{5,3},{6,4},{7,5},{8,6},{9,7},{10,8},{11,9},{12,... | collective-permute-start | bytes 2162696 | tf_op jit(solution)/shard_map/ppermute | solution.py:19
  15.8 34.6 %collective-permute-start = (bf16[352,512]{1,0:T(8,128)(2,1)S(1)}, bf16[352,512]{1,0:T(8,128)(2,1)S(1)}, u32[]{:S(2)}, u32[]{:S(2)}) collective-permute-start(bf16[352,512]{1,0:T(8,128)(2,1)S(1)} %shard_map.47), channel_id=1, source_target_pairs={{0,2},{1,3},{2,4},{3,5},{4,6},{5,7},{6,8},{7,9},{8,10},{9,11},{10,... | collective-permute-start | bytes 1081352 | tf_op jit(solution)/shard_map/ppermute | solution.py:19
  17.8 33.9 %collective-permute-start.2 = (bf16[416,512]{1,0:T(8,128)(2,1)S(1)}, bf16[416,512]{1,0:T(8,128)(2,1)S(1)}, u32[]{:S(2)}, u32[]{:S(2)}) collective-permute-start(bf16[416,512]{1,0:T(8,128)(2,1)S(1)} %get-tuple-element.9), channel_id=1, source_target_pairs={{0,2},{1,3},{2,4},{3,5},{4,6},{5,7},{6,8},{7,9},{8,10},{9,11},{10,... | collective-permute-start | bytes 1277960 | tf_op jit(solution)/shard_map/ppermute | solution.py:19
  19.7 26.9 %collective-permute-start.4 = (bf16[256,512]{1,0:T(8,128)(2,1)S(1)}, bf16[256,512]{1,0:T(8,128)(2,1)S(1)}, u32[]{:S(2)}, u32[]{:S(2)}) collective-permute-start(bf16[256,512]{1,0:T(8,128)(2,1)S(1)} %get-tuple-element.10), channel_id=1, source_target_pairs={{0,2},{1,3},{2,4},{3,5},{4,6},{5,7},{6,8},{7,9},{8,10},{9,11},{10,... | collective-permute-start | bytes 786440 | tf_op jit(solution)/shard_map/ppermute | solution.py:19
  23.8 23.2 %copy-start.2 = (bf16[1024,512]{1,0:T(8,128)(2,1)S(1)}, bf16[1024,512]{1,0:T(8,128)(2,1)}, u32[]{:S(2)}) copy-start(bf16[1024,512]{1,0:T(8,128)(2,1)} %refs_1_.1) | copy-start | bytes 3145732
  48.5 19.6 %collective-permute-start.5 = (bf16[256,512]{1,0:T(8,128)(2,1)S(1)}, bf16[256,512]{1,0:T(8,128)(2,1)S(1)}, u32[]{:S(2)}, u32[]{:S(2)}) collective-permute-start(bf16[256,512]{1,0:T(8,128)(2,1)S(1)} %convolution_convert_fusion.2), channel_id=1, source_target_pairs={{2,0},{3,1},{4,2},{5,3},{6,4},{7,5},{8,6},{9,7},{10,8},{11,9},{12,... | collective-permute-start | bytes 786440 | tf_op jit(solution)/shard_map/ppermute | solution.py:19
  53.7 12.8 %collective-permute-start.3 = (bf16[416,512]{1,0:T(8,128)(2,1)S(1)}, bf16[416,512]{1,0:T(8,128)(2,1)S(1)}, u32[]{:S(2)}, u32[]{:S(2)}) collective-permute-start(bf16[416,512]{1,0:T(8,128)(2,1)S(1)} %convolution_convert_fusion), channel_id=1, source_target_pairs={{2,0},{3,1},{4,2},{5,3},{6,4},{7,5},{8,6},{9,7},{10,8},{11,9},{12,... | collective-permute-start | bytes 1277960 | tf_op jit(solution)/shard_map/ppermute | solution.py:19

commit v4 on v1

--- a/solution.py
+++ b/solution.py
@@ -10,6 +10,7 @@
 
 PARTS = (384, 320)
 TWICE = 320
+COVER = 10**10
 
 
 def from_behind(block, axis, distance):
@@ -36,7 +37,7 @@
         copy.wait()
 
 
-def cut_rows(arrays, pieces, sizes, space):
+def cut_rows(arrays, pieces, sizes, space, flops):
     width = arrays[0].shape[1]
     vmem = pl.BlockSpec(memory_space=pltpu.VMEM)
     return pl.pallas_call(
@@ -45,6 +46,7 @@
         in_specs=[pl.BlockSpec(memory_space=space)] * len(arrays),
         out_specs=[vmem] * len(sizes),
         scratch_shapes=[pltpu.SemaphoreType.DMA((len(pieces),))],
+        cost_estimate=pl.CostEstimate(flops=flops, bytes_accessed=0, transcendentals=0),
         compiler_params=pltpu.CompilerParams(vmem_limit_bytes=2 * 2**20),
     )(*arrays)
 
@@ -54,8 +56,9 @@
     w_past = conv_weight[:width]
     w_now = conv_weight[width:]
 
-    def gradients(past, now, grad):
-        own = jnp.dot(now, w_now, preferred_element_type=jnp.float32)
+    def gradients(past, now, grad, own=None):
+        if own is None:
+            own = jnp.dot(now, w_now, preferred_element_type=jnp.float32)
         gates = own + jnp.dot(past, w_past, preferred_element_type=jnp.float32)
         tanh_part = jnp.tanh(gates[:, :width])
         sig_part = jax.nn.sigmoid(gates[:, width:])
@@ -70,17 +73,19 @@
     cuts = [(TWICE + sum(PARTS[:k]), TWICE + sum(PARTS[: k + 1])) for k in range(len(PARTS))]
     pieces = ((0, TWICE, 0, 0, PARTS[0]), (0, 0, 1, 0, TWICE), (1, 0, 1, TWICE, TWICE))
     held = [pltpu.with_memory_space_constraint(a, pltpu.HBM) for a in (signal, grad_out)]
-    part, both = cut_rows(held, pieces, (PARTS[0], 2 * TWICE), pltpu.HBM)
+    part, both = cut_rows(held, pieces, (PARTS[0], 2 * TWICE), pltpu.HBM, 0)
     past = [from_behind(part, "seq", 2)]
     ahead = from_behind(both, "seq", -2)
     pieces = ((0, cuts[1][0], 0, 0, PARTS[1]), (0, 0, 1, 0, TWICE))
-    part, head = cut_rows([signal, grad_out], pieces, (PARTS[1], TWICE), pltpu.VMEM)
+    part, head = cut_rows([signal, grad_out], pieces, (PARTS[1], TWICE), pltpu.VMEM, COVER)
     past.append(from_behind(part, "seq", 2))
+    own = jnp.dot(signal[cuts[0][0] : cuts[0][1]], w_now, preferred_element_type=jnp.float32)
+    own, head = lax.optimization_barrier((own, head))
     past_both = from_behind(head, "seq", 2)
     accs = []
     backs = []
     for k, (a, b) in enumerate(cuts):
-        d_gates = gradients(past[k], signal[a:b], grad_out[a:b])
+        d_gates = gradients(past[k], signal[a:b], grad_out[a:b], own if k == 0 else None)
         backs.append(from_behind(far_of(d_gates), "seq", -2))
         acc = grad_out[a:b].astype(jnp.float32) + contract_rows(d_gates, w_now)
         accs.append(lax.optimization_barrier(acc))

time: 57.7 us -> 64.4 us (1.12)
  waiting for transfers between devices: 13 us -> 25.5 us
  starting transfers between devices: 27.6 us -> 24.2 us
  local copies, waits for them, and re-layouts: 2.53 us -> 0.02 us
    ppermute x6, waiting for transfers between devices: 13 us -> 25.5 us  [from_behind(): return lax.ppermute(block, axis, route)]
    ppermute x6, starting transfers between devices: 27.6 us -> 24.2 us  [from_behind(): return lax.ppermute(block, axis, route)]
    unnamed x12 -> x8, local copies, waits for them, and re-layouts: 2.53 us -> 0.02 us
    dot_general x4 -> x3, matrix products: 2.14 us -> 1.55 us  [gradients(): own = jnp.dot(now, w_now, preferred_element_type=jnp.float32)]
  transfers between devices with their start and end apart: 6 -> 6, of which waited for: 3 -> 2; matrix products, arithmetic and copies ran while one was open for 20% -> 18% of each run, Pallas kernels for 2% -> 0%
where the time goes in v4:
time: 64.4 us; the launch traced here: 64.2 us
  waiting for transfers between devices  25.5 us (40%)
  starting transfers between devices  24.2 us (38%)
  matrix products  10 us (16%)
  other arithmetic  2.58 us (4%)
  Pallas kernels  1.59 us (2%)
    ppermute x6, waiting for transfers between devices, from_behind(): return lax.ppermute(block, axis, route)  25.5 us
    ppermute x6, starting transfers between devices, from_behind(): return lax.ppermute(block, axis, route)  24.2 us
    dot_general x10, matrix products, contract_rows(): lax.dot_general(left, right, (((1,), (1,)), ((), ())), preferred_element_...  5.75 us
    dot_general x4, matrix products, gradients(): gates = own + jnp.dot(past, w_past, preferred_element_type=jnp.float32)  2.11 us
    pallas_call x2, Pallas kernels, cut_rows(): pl.pallas_call(functools.partial(cut_body, pieces), out_shape=[jax.ShapeD...  1.59 us
    concatenate x1, other arithmetic, shards(): out = jnp.concatenate([first, *mids, accs[-1]], 0)  1.55 us
    dot_general x3, matrix products, gradients(): own = jnp.dot(now, w_now, preferred_element_type=jnp.float32)  1.55 us
  transfers between devices with their start and end apart: 6, of which 2 were waited for; matrix products, arithmetic and copies ran while one was open for 18% of the time, Pallas kernels for 0%

profile of v4, /device:TPU:6, one launch (start us, length us, event | category | flops | bytes accessed | tf_op | source)
XLA Modules:
  0.0 64.2 jit_solution(9339290975035946408)
XLA Ops:
  0.0 0.0 copy-start
  0.0 0.0 copy-start.1
  0.0 0.0 copy-start.2
  0.0 1.4 %shard_map.47 = (bf16[384,512]{1,0:T(8,128)(2,1)S(1)}, bf16[640,512]{1,0:T(8,128)(2,1)S(1)}) custom-call(bf16[1024,512]{1,0:T(8,128)(2,1)} %refs_0_.3, bf16[1024,512]{1,0:T(8,128)(2,1)} %refs_1_.3), custom_call_target="tpu_custom_call" | custom-call | tf_op jit(solution)/shard_map/pallas_call | solution.py:43
  1.4 3.5 %collective-permute-start.2 = (bf16[384,512]{1,0:T(8,128)(2,1)S(1)}, bf16[384,512]{1,0:T(8,128)(2,1)S(1)}, u32[]{:S(2)}, u32[]{:S(2)}) collective-permute-start(bf16[384,512]{1,0:T(8,128)(2,1)S(1)} %get-tuple-element.15), channel_id=1, source_target_pairs={{0,2},{1,3},{2,4},{3,5},{4,6},{5,7},{6,8},{7,9},{8,10},{9,11},{10,... | collective-permute-start | bytes 1179656 | tf_op jit(solution)/shard_map/ppermute | solution.py:19
  4.9 0.0 copy-start.3
  4.9 12.7 %collective-permute-start.1 = (bf16[640,512]{1,0:T(8,128)(2,1)S(1)}, bf16[640,512]{1,0:T(8,128)(2,1)S(1)}, u32[]{:S(2)}, u32[]{:S(2)}) collective-permute-start(bf16[640,512]{1,0:T(8,128)(2,1)S(1)} %get-tuple-element.13), channel_id=1, source_target_pairs={{2,0},{3,1},{4,2},{5,3},{6,4},{7,5},{8,6},{9,7},{10,8},{11,9},{12,... | collective-permute-start | bytes 1966088 | tf_op jit(solution)/shard_map/ppermute | solution.py:19
  17.6 0.0 copy-done.1
  17.6 0.0 copy-done.2
  17.6 0.2 shard_map.46
  17.8 0.0 copy-done.3
  17.8 0.6 fusion.20
  18.4 1.9 %collective-permute-start = (bf16[320,512]{1,0:T(8,128)(2,1)S(1)}, bf16[320,512]{1,0:T(8,128)(2,1)S(1)}, u32[]{:S(2)}, u32[]{:S(2)}) collective-permute-start(bf16[320,512]{1,0:T(8,128)(2,1)S(1)} %get-tuple-element.12), channel_id=1, source_target_pairs={{0,2},{1,3},{2,4},{3,5},{4,6},{5,7},{6,8},{7,9},{8,10},{9,11},{10,... | collective-permute-start | bytes 983048 | tf_op jit(solution)/shard_map/ppermute | solution.py:19
  20.4 1.9 %collective-permute-start.4 = (bf16[320,512]{1,0:T(8,128)(2,1)S(1)}, bf16[320,512]{1,0:T(8,128)(2,1)S(1)}, u32[]{:S(2)}, u32[]{:S(2)}) collective-permute-start(bf16[320,512]{1,0:T(8,128)(2,1)S(1)} %get-tuple-element.16), channel_id=1, source_target_pairs={{0,2},{1,3},{2,4},{3,5},{4,6},{5,7},{6,8},{7,9},{8,10},{9,11},{10,... | collective-permute-start | bytes 983048 | tf_op jit(solution)/shard_map/ppermute | solution.py:19
  22.3 0.5 fusion.34
  22.8 0.5 fusion.43
  23.4 0.5 fusion.27
  23.9 16.9 %collective-permute-done.4 = bf16[320,512]{1,0:T(8,128)(2,1)S(1)} collective-permute-done((bf16[320,512]{1,0:T(8,128)(2,1)S(1)}, bf16[320,512]{1,0:T(8,128)(2,1)S(1)}, u32[]{:S(2)}, u32[]{:S(2)}) %collective-permute-start.4) | collective-permute-done | bytes 327712 | tf_op jit(solution)/shard_map/ppermute | solution.py:19
  40.7 0.5 convolution_add_fusion.1
  41.3 0.0 copy-done
  41.3 0.6 multiply_convert_fusion.3
  41.9 0.5 convolution_add_fusion.5
  42.4 0.5 convolution_convert_fusion.1
  43.0 1.9 %collective-permute-start.5 = (bf16[320,512]{1,0:T(8,128)(2,1)S(1)}, bf16[320,512]{1,0:T(8,128)(2,1)S(1)}, u32[]{:S(2)}, u32[]{:S(2)}) collective-permute-start(bf16[320,512]{1,0:T(8,128)(2,1)S(1)} %convolution_convert_fusion.1), channel_id=1, source_target_pairs={{2,0},{3,1},{4,2},{5,3},{6,4},{7,5},{8,6},{9,7},{10,8},{11,9},{12,... | collective-permute-start | bytes 983048 | tf_op jit(solution)/shard_map/ppermute | solution.py:19
  44.9 0.0 collective-permute-done
  44.9 0.5 convolution_add_fusion.3
  45.4 0.6 multiply_convert_fusion.7
  46.0 0.0 collective-permute-done.2
  46.0 0.6 convolution_add_fusion
  46.6 0.7 %multiply_convert_fusion.1 = (bf16[384,512]{1,0:T(8,128)(2,1)S(1)}, bf16[384,512]{1,0:T(8,128)(2,1)S(1)}) fusion(f32[384,1024]{1,0:T(8,128)S(1)} %convolution_add_fusion, bf16[512,512]{1,0:T(8,128)(2,1)S(1)} %copy-done, bf16[1024,512]{1,0:T(8,128)(2,1)S(1)} %copy-done.2), kind=kOutput, calls=%fused_computation.21 | convolution fusion | flops 203882496 | bytes 3276800 | tf_op jit(solution)/shard_map/dot_general | solution.py:23
  47.2 0.6 convolution_convert_fusion
  47.9 2.3 %collective-permute-start.3 = (bf16[384,512]{1,0:T(8,128)(2,1)S(1)}, bf16[384,512]{1,0:T(8,128)(2,1)S(1)}, u32[]{:S(2)}, u32[]{:S(2)}) collective-permute-start(bf16[384,512]{1,0:T(8,128)(2,1)S(1)} %convolution_convert_fusion), channel_id=1, source_target_pairs={{2,0},{3,1},{4,2},{5,3},{6,4},{7,5},{8,6},{9,7},{10,8},{11,9},{12,... | collective-permute-start | bytes 1179656 | tf_op jit(solution)/shard_map/ppermute | solution.py:19
  50.1 0.6 convolution_add_fusion.4
  50.8 0.0 collective-permute-done.1
  50.8 0.5 convolution_add_fusion.2
  51.3 0.6 multiply_convert_fusion.5
  51.9 0.5 fusion.1
  52.4 0.5 fusion
  53.0 8.6 %collective-permute-done.3 = bf16[384,512]{1,0:T(8,128)(2,1)S(1)} collective-permute-done((bf16[384,512]{1,0:T(8,128)(2,1)S(1)}, bf16[384,512]{1,0:T(8,128)(2,1)S(1)}, u32[]{:S(2)}, u32[]{:S(2)}) %collective-permute-start.3) | collective-permute-done | bytes 393248 | tf_op jit(solution)/shard_map/ppermute | solution.py:19
  61.6 0.1 convert_add_fusion
  61.7 1.6 %pad_maximum_fusion = f32[1024,512]{1,0:T(8,128)} fusion(f32[320,512]{1,0:T(8,128)S(1)} %convolution_add_fusion.5, f32[384,512]{1,0:T(8,128)S(1)} %convert_add_fusion, f32[320,512]{1,0:T(8,128)S(1)} %fusion), kind=kLoop, calls=%fused_computation | loop fusion | flops 1048576 | bytes 4194304 | tf_op jit(solution)/shard_map/concatenate | solution.py:97
  63.2 0.0 collective-permute-done.5
  63.3 0.9 %add_dynamic-update-slice_fusion = f32[1024,512]{1,0:T(8,128)} fusion(f32[1024,512]{1,0:T(8,128)} %pad_maximum_fusion, f32[320,512]{1,0:T(8,128)S(1)} %convolution_add_fusion.5, bf16[320,512]{1,0:T(8,128)(2,1)S(1)} %collective-permute-done.5), kind=kLoop, calls=%fused_computation.44 | loop fusion | flops 327680 | bytes 1638400 | tf_op jit(solution)/shard_map/dynamic_update_slice | solution.py:99
Async XLA Ops:
  0.0 41.3 %copy-start = (bf16[512,512]{1,0:T(8,128)(2,1)S(1)}, bf16[512,512]{1,0:T(8,128)(2,1)}, u32[]{:S(2)}) copy-start(bf16[512,512]{1,0:T(8,128)(2,1)} %param.7) | copy-start | bytes 1572868
  0.0 17.6 %copy-start.1 = (bf16[1024,512]{1,0:T(8,128)(2,1)S(1)}, bf16[1024,512]{1,0:T(8,128)(2,1)}, u32[]{:S(2)}) copy-start(bf16[1024,512]{1,0:T(8,128)(2,1)} %refs_0_.3) | copy-start | bytes 3145732
  0.0 17.6 %copy-start.2 = (bf16[1024,512]{1,0:T(8,128)(2,1)S(1)}, bf16[1024,512]{1,0:T(8,128)(2,1)}, u32[]{:S(2)}) copy-start(bf16[1024,512]{1,0:T(8,128)(2,1)} %refs_1_.3) | copy-start | bytes 3145732
  1.4 44.6 %collective-permute-start.2 = (bf16[384,512]{1,0:T(8,128)(2,1)S(1)}, bf16[384,512]{1,0:T(8,128)(2,1)S(1)}, u32[]{:S(2)}, u32[]{:S(2)}) collective-permute-start(bf16[384,512]{1,0:T(8,128)(2,1)S(1)} %get-tuple-element.15), channel_id=1, source_target_pairs={{0,2},{1,3},{2,4},{3,5},{4,6},{5,7},{6,8},{7,9},{8,10},{9,11},{10,... | collective-permute-start | bytes 1179656 | tf_op jit(solution)/shard_map/ppermute | solution.py:19
  4.9 13.0 %copy-start.3 = (bf16[1024,1024]{1,0:T(8,128)(2,1)S(1)}, bf16[1024,1024]{1,0:T(8,128)(2,1)}, u32[]{:S(2)}) copy-start(bf16[1024,1024]{1,0:T(8,128)(2,1)} %param.6) | copy-start | bytes 6291460
  4.9 45.9 %collective-permute-start.1 = (bf16[640,512]{1,0:T(8,128)(2,1)S(1)}, bf16[640,512]{1,0:T(8,128)(2,1)S(1)}, u32[]{:S(2)}, u32[]{:S(2)}) collective-permute-start(bf16[640,512]{1,0:T(8,128)(2,1)S(1)} %get-tuple-element.13), channel_id=1, source_target_pairs={{2,0},{3,1},{4,2},{5,3},{6,4},{7,5},{8,6},{9,7},{10,8},{11,9},{12,... | collective-permute-start | bytes 1966088 | tf_op jit(solution)/shard_map/ppermute | solution.py:19
  18.4 26.4 %collective-permute-start = (bf16[320,512]{1,0:T(8,128)(2,1)S(1)}, bf16[320,512]{1,0:T(8,128)(2,1)S(1)}, u32[]{:S(2)}, u32[]{:S(2)}) collective-permute-start(bf16[320,512]{1,0:T(8,128)(2,1)S(1)} %get-tuple-element.12), channel_id=1, source_target_pairs={{0,2},{1,3},{2,4},{3,5},{4,6},{5,7},{6,8},{7,9},{8,10},{9,11},{10,... | collective-permute-start | bytes 983048 | tf_op jit(solution)/shard_map/ppermute | solution.py:19
  20.4 20.4 %collective-permute-start.4 = (bf16[320,512]{1,0:T(8,128)(2,1)S(1)}, bf16[320,512]{1,0:T(8,128)(2,1)S(1)}, u32[]{:S(2)}, u32[]{:S(2)}) collective-permute-start(bf16[320,512]{1,0:T(8,128)(2,1)S(1)} %get-tuple-element.16), channel_id=1, source_target_pairs={{0,2},{1,3},{2,4},{3,5},{4,6},{5,7},{6,8},{7,9},{8,10},{9,11},{10,... | collective-permute-start | bytes 983048 | tf_op jit(solution)/shard_map/ppermute | solution.py:19
  43.0 20.3 %collective-permute-start.5 = (bf16[320,512]{1,0:T(8,128)(2,1)S(1)}, bf16[320,512]{1,0:T(8,128)(2,1)S(1)}, u32[]{:S(2)}, u32[]{:S(2)}) collective-permute-start(bf16[320,512]{1,0:T(8,128)(2,1)S(1)} %convolution_convert_fusion.1), channel_id=1, source_target_pairs={{2,0},{3,1},{4,2},{5,3},{6,4},{7,5},{8,6},{9,7},{10,8},{11,9},{12,... | collective-permute-start | bytes 983048 | tf_op jit(solution)/shard_map/ppermute | solution.py:19
  47.9 13.7 %collective-permute-start.3 = (bf16[384,512]{1,0:T(8,128)(2,1)S(1)}, bf16[384,512]{1,0:T(8,128)(2,1)S(1)}, u32[]{:S(2)}, u32[]{:S(2)}) collective-permute-start(bf16[384,512]{1,0:T(8,128)(2,1)S(1)} %convolution_convert_fusion), channel_id=1, source_target_pairs={{2,0},{3,1},{4,2},{5,3},{6,4},{7,5},{8,6},{9,7},{10,8},{11,9},{12,... | collective-permute-start | bytes 1179656 | tf_op jit(solution)/shard_map/ppermute | solution.py:19

commit v5 on v1

--- a/solution.py
+++ b/solution.py
@@ -8,8 +8,9 @@
 from jax.sharding import PartitionSpec as P
 
 
-PARTS = (384, 320)
+PARTS = (400, 304)
 TWICE = 320
+COVER = 10**10
 
 
 def from_behind(block, axis, distance):
@@ -36,7 +37,7 @@
         copy.wait()
 
 
-def cut_rows(arrays, pieces, sizes, space):
+def cut_rows(arrays, pieces, sizes, space, flops):
     width = arrays[0].shape[1]
     vmem = pl.BlockSpec(memory_space=pltpu.VMEM)
     return pl.pallas_call(
@@ -45,6 +46,7 @@
         in_specs=[pl.BlockSpec(memory_space=space)] * len(arrays),
         out_specs=[vmem] * len(sizes),
         scratch_shapes=[pltpu.SemaphoreType.DMA((len(pieces),))],
+        cost_estimate=pl.CostEstimate(flops=flops, bytes_accessed=0, transcendentals=0),
         compiler_params=pltpu.CompilerParams(vmem_limit_bytes=2 * 2**20),
     )(*arrays)
 
@@ -70,11 +72,11 @@
     cuts = [(TWICE + sum(PARTS[:k]), TWICE + sum(PARTS[: k + 1])) for k in range(len(PARTS))]
     pieces = ((0, TWICE, 0, 0, PARTS[0]), (0, 0, 1, 0, TWICE), (1, 0, 1, TWICE, TWICE))
     held = [pltpu.with_memory_space_constraint(a, pltpu.HBM) for a in (signal, grad_out)]
-    part, both = cut_rows(held, pieces, (PARTS[0], 2 * TWICE), pltpu.HBM)
+    part, both = cut_rows(held, pieces, (PARTS[0], 2 * TWICE), pltpu.HBM, 0)
     past = [from_behind(part, "seq", 2)]
     ahead = from_behind(both, "seq", -2)
     pieces = ((0, cuts[1][0], 0, 0, PARTS[1]), (0, 0, 1, 0, TWICE))
-    part, head = cut_rows([signal, grad_out], pieces, (PARTS[1], TWICE), pltpu.VMEM)
+    part, head = cut_rows([signal, grad_out], pieces, (PARTS[1], TWICE), pltpu.VMEM, COVER)
     past.append(from_behind(part, "seq", 2))
     past_both = from_behind(head, "seq", 2)
     accs = []

time: 57.7 us -> 58.1 us (level)
  local copies, waits for them, and re-layouts: 2.53 us -> 3.22 us
    unnamed x12, local copies, waits for them, and re-layouts: 2.53 us -> 3.22 us
  transfers between devices with their start and end apart: 6 -> 6, of which waited for: 3 -> 2; matrix products, arithmetic and copies ran while one was open for 20% -> 20% of each run, Pallas kernels for 2% -> 2%
where the time goes in v5:
time: 58.1 us; the launch traced here: 57.8 us
  starting transfers between devices  27.6 us (48%)
  waiting for transfers between devices  12.7 us (22%)
  matrix products  10.1 us (17%)
  local copies, waits for them, and re-layouts  3.22 us (6%)
  other arithmetic  2.57 us (4%)
  Pallas kernels  1.42 us (2%)
    ppermute x6, starting transfers between devices, from_behind(): return lax.ppermute(block, axis, route)  27.6 us
    ppermute x6, waiting for transfers between devices, from_behind(): return lax.ppermute(block, axis, route)  12.7 us
    dot_general x10, matrix products, contract_rows(): lax.dot_general(left, right, (((1,), (1,)), ((), ())), preferred_element_...  5.75 us
    unnamed x12, local copies, waits for them, and re-layouts  3.22 us
    dot_general x4, matrix products, gradients(): gates = own + jnp.dot(past, w_past, preferred_element_type=jnp.float32)  2.18 us
    dot_general x4, matrix products, gradients(): own = jnp.dot(now, w_now, preferred_element_type=jnp.float32)  2.14 us
    concatenate x1, other arithmetic, shards(): out = jnp.concatenate([first, *mids, accs[-1]], 0)  1.55 us
    pallas_call x2, Pallas kernels, cut_rows(): pl.pallas_call(functools.partial(cut_body, pieces), out_shape=[jax.ShapeD...  1.42 us
  transfers between devices with their start and end apart: 6, of which 2 were waited for; matrix products, arithmetic and copies ran while one was open for 20% of the time, Pallas kernels for 2%

profile of v5, /device:TPU:6, one launch (start us, length us, event | category | flops | bytes accessed | tf_op | source)
XLA Modules:
  0.0 57.8 jit_solution(672548110107274591)
XLA Ops:
  0.0 0.0 copy-start
  0.0 0.0 copy-start.1
  0.0 1.3 %copy-done.1 = bf16[1024,512]{1,0:T(8,128)(2,1)S(1)} copy-done((bf16[1024,512]{1,0:T(8,128)(2,1)S(1)}, bf16[1024,512]{1,0:T(8,128)(2,1)}, u32[]{:S(2)}) %copy-start.1) | copy-done | bytes 1048600
  1.3 0.0 copy-start.3
  1.3 1.2 %copy-done.3 = bf16[1024,512]{1,0:T(8,128)(2,1)S(1)} copy-done((bf16[1024,512]{1,0:T(8,128)(2,1)S(1)}, bf16[1024,512]{1,0:T(8,128)(2,1)}, u32[]{:S(2)}) %copy-start.3) | copy-done | bytes 1048600
  2.5 0.0 copy-start.5
  2.5 0.2 shard_map.46
  2.7 0.0 copy-start.2
  2.7 3.6 %collective-permute-start.4 = (bf16[304,512]{1,0:T(8,128)(2,1)S(1)}, bf16[304,512]{1,0:T(8,128)(2,1)S(1)}, u32[]{:S(2)}, u32[]{:S(2)}) collective-permute-start(bf16[304,512]{1,0:T(8,128)(2,1)S(1)} %get-tuple-element.12), channel_id=1, source_target_pairs={{0,2},{1,3},{2,4},{3,5},{4,6},{5,7},{6,8},{7,9},{8,10},{9,11},{10,... | collective-permute-start | bytes 933896 | tf_op jit(solution)/shard_map/ppermute | solution.py:19
  6.4 3.5 %collective-permute-start = (bf16[320,512]{1,0:T(8,128)(2,1)S(1)}, bf16[320,512]{1,0:T(8,128)(2,1)S(1)}, u32[]{:S(2)}, u32[]{:S(2)}) collective-permute-start(bf16[320,512]{1,0:T(8,128)(2,1)S(1)} %get-tuple-element.9), channel_id=1, source_target_pairs={{0,2},{1,3},{2,4},{3,5},{4,6},{5,7},{6,8},{7,9},{8,10},{9,11},{10,... | collective-permute-start | bytes 983048 | tf_op jit(solution)/shard_map/ppermute | solution.py:19
  9.8 1.2 %shard_map.47 = (bf16[400,512]{1,0:T(8,128)(2,1)S(1)}, bf16[640,512]{1,0:T(8,128)(2,1)S(1)}) custom-call(bf16[1024,512]{1,0:T(8,128)(2,1)} %refs_0_.3, bf16[1024,512]{1,0:T(8,128)(2,1)} %refs_1_.3), custom_call_target="tpu_custom_call" | custom-call | tf_op jit(solution)/shard_map/pallas_call | solution.py:43
  11.1 3.2 %collective-permute-start.2 = (bf16[400,512]{1,0:T(8,128)(2,1)S(1)}, bf16[400,512]{1,0:T(8,128)(2,1)S(1)}, u32[]{:S(2)}, u32[]{:S(2)}) collective-permute-start(bf16[400,512]{1,0:T(8,128)(2,1)S(1)} %get-tuple-element.11), channel_id=1, source_target_pairs={{0,2},{1,3},{2,4},{3,5},{4,6},{5,7},{6,8},{7,9},{8,10},{9,11},{10,... | collective-permute-start | bytes 1228808 | tf_op jit(solution)/shard_map/ppermute | solution.py:19
  14.3 9.7 %collective-permute-start.1 = (bf16[640,512]{1,0:T(8,128)(2,1)S(1)}, bf16[640,512]{1,0:T(8,128)(2,1)S(1)}, u32[]{:S(2)}, u32[]{:S(2)}) collective-permute-start(bf16[640,512]{1,0:T(8,128)(2,1)S(1)} %get-tuple-element.10), channel_id=1, source_target_pairs={{2,0},{3,1},{4,2},{5,3},{6,4},{7,5},{8,6},{9,7},{10,8},{11,9},{12,... | collective-permute-start | bytes 1966088 | tf_op jit(solution)/shard_map/ppermute | solution.py:19
  24.0 0.0 copy-done.5
  24.0 0.0 copy-done.2
  24.0 0.5 fusion.34
  24.6 0.5 fusion.43
  25.1 0.5 fusion.27
  25.6 0.6 %fusion.20 = f32[400,1024]{1,0:T(8,128)S(1)} fusion(bf16[1024,512]{1,0:T(8,128)(2,1)S(1)} %copy-done.2, bf16[1024,1024]{1,0:T(8,128)(2,1)S(1)} %copy-done.5), kind=kOutput, calls=%fused_computation.51 | convolution fusion | flops 419430400 | bytes 3096576 | tf_op jit(solution)/shard_map/dot_general | solution.py:60
  26.2 0.0 copy-start.4
  26.2 0.0 collective-permute-done.4
  26.2 0.5 convolution_add_fusion.3
  26.7 0.0 copy-done
  26.7 0.7 %copy-done.4 = bf16[1024,512]{1,0:T(8,128)(2,1)S(1)} copy-done((bf16[1024,512]{1,0:T(8,128)(2,1)S(1)}, bf16[1024,512]{1,0:T(8,128)(2,1)}, u32[]{:S(2)}) %copy-start.4) | copy-done | bytes 1048600
  27.4 0.6 multiply_convert_fusion.7
  28.0 0.5 convolution_add_fusion.6
  28.5 0.5 convolution_convert_fusion.2
  29.1 3.9 %collective-permute-start.5 = (bf16[304,512]{1,0:T(8,128)(2,1)S(1)}, bf16[304,512]{1,0:T(8,128)(2,1)S(1)}, u32[]{:S(2)}, u32[]{:S(2)}) collective-permute-start(bf16[304,512]{1,0:T(8,128)(2,1)S(1)} %convolution_convert_fusion.2), channel_id=1, source_target_pairs={{2,0},{3,1},{4,2},{5,3},{6,4},{7,5},{8,6},{9,7},{10,8},{11,9},{12,... | collective-permute-start | bytes 933896 | tf_op jit(solution)/shard_map/ppermute | solution.py:19
  33.0 0.0 collective-permute-done
  33.0 0.5 convolution_add_fusion.2
  33.5 0.6 multiply_convert_fusion.5
  34.1 6.0 %collective-permute-done.2 = bf16[400,512]{1,0:T(8,128)(2,1)S(1)} collective-permute-done((bf16[400,512]{1,0:T(8,128)(2,1)S(1)}, bf16[400,512]{1,0:T(8,128)(2,1)S(1)}, u32[]{:S(2)}, u32[]{:S(2)}) %collective-permute-start.2) | collective-permute-done | bytes 409632 | tf_op jit(solution)/shard_map/ppermute | solution.py:19
  40.1 0.6 %convolution_add_fusion = f32[400,1024]{1,0:T(8,128)S(1)} fusion(f32[400,1024]{1,0:T(8,128)S(1)} %fusion.20, bf16[400,512]{1,0:T(8,128)(2,1)S(1)} %collective-permute-done.2, bf16[1024,1024]{1,0:T(8,128)(2,1)S(1)} %copy-done.5), kind=kOutput, calls=%fused_computation.1 | convolution fusion | flops 419840000 | bytes 4734976 | tf_op jit(solution)/shard_map/dot_general | solution.py:61
  40.8 0.7 %multiply_convert_fusion.1 = (bf16[400,512]{1,0:T(8,128)(2,1)S(1)}, bf16[400,512]{1,0:T(8,128)(2,1)S(1)}) fusion(f32[400,1024]{1,0:T(8,128)S(1)} %convolution_add_fusion, bf16[512,512]{1,0:T(8,128)(2,1)S(1)} %copy-done, bf16[1024,512]{1,0:T(8,128)(2,1)S(1)} %copy-done.4), kind=kOutput, calls=%fused_computation.21 | convolution fusion | flops 212377600 | bytes 3391488 | tf_op jit(solution)/shard_map/dot_general | solution.py:23
  41.5 0.6 %convolution_add_fusion.4 = f32[400,512]{1,0:T(8,128)S(1)} fusion(bf16[400,512]{1,0:T(8,128)(2,1)S(1)} %get-tuple-element.14, bf16[400,512]{1,0:T(8,128)(2,1)S(1)} %get-tuple-element.13, bf16[1024,512]{1,0:T(8,128)(2,1)S(1)} %copy-done.4, bf16[1024,1024]{1,0:T(8,128)(2,1)S(1)} %copy-done.5), kind=kOutput, calls=%fused_computation.5 | convolution fusion | flops 421478400 | bytes 3096576 | tf_op jit(solution)/shard_map/dot_general | solution.py:23
  42.1 0.6 %convolution_convert_fusion = bf16[400,512]{1,0:T(8,128)(2,1)S(1)} fusion(bf16[400,512]{1,0:T(8,128)(2,1)S(1)} %get-tuple-element.14, bf16[400,512]{1,0:T(8,128)(2,1)S(1)} %get-tuple-element.13, bf16[1024,1024]{1,0:T(8,128)(2,1)S(1)} %copy-done.5), kind=kOutput, calls=%fused_computation.9 | convolution fusion | flops 421273600 | bytes 2277376 | tf_op jit(solution)/shard_map/dot_general | solution.py:23
  42.7 3.6 %collective-permute-start.3 = (bf16[400,512]{1,0:T(8,128)(2,1)S(1)}, bf16[400,512]{1,0:T(8,128)(2,1)S(1)}, u32[]{:S(2)}, u32[]{:S(2)}) collective-permute-start(bf16[400,512]{1,0:T(8,128)(2,1)S(1)} %convolution_convert_fusion), channel_id=1, source_target_pairs={{2,0},{3,1},{4,2},{5,3},{6,4},{7,5},{8,6},{9,7},{10,8},{11,9},{12,... | collective-permute-start | bytes 1228808 | tf_op jit(solution)/shard_map/ppermute | solution.py:19
  46.4 0.0 collective-permute-done.1
  46.4 0.5 convolution_add_fusion.1
  46.9 0.6 multiply_convert_fusion.3
  47.5 0.5 fusion.1
  48.0 0.5 fusion
  48.6 6.7 %collective-permute-done.3 = bf16[400,512]{1,0:T(8,128)(2,1)S(1)} collective-permute-done((bf16[400,512]{1,0:T(8,128)(2,1)S(1)}, bf16[400,512]{1,0:T(8,128)(2,1)S(1)}, u32[]{:S(2)}, u32[]{:S(2)}) %collective-permute-start.3) | collective-permute-done | bytes 409632 | tf_op jit(solution)/shard_map/ppermute | solution.py:19
  55.2 0.1 convert_add_fusion
  55.4 1.6 %pad_maximum_fusion = f32[1024,512]{1,0:T(8,128)} fusion(f32[304,512]{1,0:T(8,128)S(1)} %convolution_add_fusion.6, f32[400,512]{1,0:T(8,128)S(1)} %convert_add_fusion, f32[320,512]{1,0:T(8,128)S(1)} %fusion), kind=kLoop, calls=%fused_computation | loop fusion | flops 1048576 | bytes 4194304 | tf_op jit(solution)/shard_map/concatenate | solution.py:94
  56.9 0.0 collective-permute-done.5
  56.9 0.9 %add_dynamic-update-slice_fusion = f32[1024,512]{1,0:T(8,128)} fusion(f32[1024,512]{1,0:T(8,128)} %pad_maximum_fusion, f32[304,512]{1,0:T(8,128)S(1)} %convolution_add_fusion.6, bf16[304,512]{1,0:T(8,128)(2,1)S(1)} %collective-permute-done.5), kind=kLoop, calls=%fused_computation.48 | loop fusion | flops 311296 | bytes 1556480 | tf_op jit(solution)/shard_map/dynamic_update_slice | solution.py:96
Async XLA Ops:
  0.0 26.7 %copy-start = (bf16[512,512]{1,0:T(8,128)(2,1)S(1)}, bf16[512,512]{1,0:T(8,128)(2,1)}, u32[]{:S(2)}) copy-start(bf16[512,512]{1,0:T(8,128)(2,1)} %param.7) | copy-start | bytes 1572868
  0.0 1.3 %copy-start.1 = (bf16[1024,512]{1,0:T(8,128)(2,1)S(1)}, bf16[1024,512]{1,0:T(8,128)(2,1)}, u32[]{:S(2)}) copy-start(bf16[1024,512]{1,0:T(8,128)(2,1)} %refs_0_.3) | copy-start | bytes 3145732
  1.3 1.2 %copy-start.3 = (bf16[1024,512]{1,0:T(8,128)(2,1)S(1)}, bf16[1024,512]{1,0:T(8,128)(2,1)}, u32[]{:S(2)}) copy-start(bf16[1024,512]{1,0:T(8,128)(2,1)} %refs_1_.3) | copy-start | bytes 3145732
  2.5 21.5 %copy-start.5 = (bf16[1024,1024]{1,0:T(8,128)(2,1)S(1)}, bf16[1024,1024]{1,0:T(8,128)(2,1)}, u32[]{:S(2)}) copy-start(bf16[1024,1024]{1,0:T(8,128)(2,1)} %param.6) | copy-start | bytes 6291460
  2.7 21.3 %copy-start.2 = (bf16[1024,512]{1,0:T(8,128)(2,1)S(1)}, bf16[1024,512]{1,0:T(8,128)(2,1)}, u32[]{:S(2)}) copy-start(bf16[1024,512]{1,0:T(8,128)(2,1)} %refs_0_.3) | copy-start | bytes 3145732
  2.7 23.5 %collective-permute-start.4 = (bf16[304,512]{1,0:T(8,128)(2,1)S(1)}, bf16[304,512]{1,0:T(8,128)(2,1)S(1)}, u32[]{:S(2)}, u32[]{:S(2)}) collective-permute-start(bf16[304,512]{1,0:T(8,128)(2,1)S(1)} %get-tuple-element.12), channel_id=1, source_target_pairs={{0,2},{1,3},{2,4},{3,5},{4,6},{5,7},{6,8},{7,9},{8,10},{9,11},{10,... | collective-permute-start | bytes 933896 | tf_op jit(solution)/shard_map/ppermute | solution.py:19
  6.4 26.6 %collective-permute-start = (bf16[320,512]{1,0:T(8,128)(2,1)S(1)}, bf16[320,512]{1,0:T(8,128)(2,1)S(1)}, u32[]{:S(2)}, u32[]{:S(2)}) collective-permute-start(bf16[320,512]{1,0:T(8,128)(2,1)S(1)} %get-tuple-element.9), channel_id=1, source_target_pairs={{0,2},{1,3},{2,4},{3,5},{4,6},{5,7},{6,8},{7,9},{8,10},{9,11},{10,... | collective-permute-start | bytes 983048 | tf_op jit(solution)/shard_map/ppermute | solution.py:19
  11.1 29.1 %collective-permute-start.2 = (bf16[400,512]{1,0:T(8,128)(2,1)S(1)}, bf16[400,512]{1,0:T(8,128)(2,1)S(1)}, u32[]{:S(2)}, u32[]{:S(2)}) collective-permute-start(bf16[400,512]{1,0:T(8,128)(2,1)S(1)} %get-tuple-element.11), channel_id=1, source_target_pairs={{0,2},{1,3},{2,4},{3,5},{4,6},{5,7},{6,8},{7,9},{8,10},{9,11},{10,... | collective-permute-start | bytes 1228808 | tf_op jit(solution)/shard_map/ppermute | solution.py:19
  14.3 32.1 %collective-permute-start.1 = (bf16[640,512]{1,0:T(8,128)(2,1)S(1)}, bf16[640,512]{1,0:T(8,128)(2,1)S(1)}, u32[]{:S(2)}, u32[]{:S(2)}) collective-permute-start(bf16[640,512]{1,0:T(8,128)(2,1)S(1)} %get-tuple-element.10), channel_id=1, source_target_pairs={{2,0},{3,1},{4,2},{5,3},{6,4},{7,5},{8,6},{9,7},{10,8},{11,9},{12,... | collective-permute-start | bytes 1966088 | tf_op jit(solution)/shard_map/ppermute | solution.py:19
  26.2 1.2 %copy-start.4 = (bf16[1024,512]{1,0:T(8,128)(2,1)S(1)}, bf16[1024,512]{1,0:T(8,128)(2,1)}, u32[]{:S(2)}) copy-start(bf16[1024,512]{1,0:T(8,128)(2,1)} %refs_1_.3) | copy-start | bytes 3145732
  29.1 27.9 %collective-permute-start.5 = (bf16[304,512]{1,0:T(8,128)(2,1)S(1)}, bf16[304,512]{1,0:T(8,128)(2,1)S(1)}, u32[]{:S(2)}, u32[]{:S(2)}) collective-permute-start(bf16[304,512]{1,0:T(8,128)(2,1)S(1)} %convolution_convert_fusion.2), channel_id=1, source_target_pairs={{2,0},{3,1},{4,2},{5,3},{6,4},{7,5},{8,6},{9,7},{10,8},{11,9},{12,... | collective-permute-start | bytes 933896 | tf_op jit(solution)/shard_map/ppermute | solution.py:19
  42.7 12.5 %collective-permute-start.3 = (bf16[400,512]{1,0:T(8,128)(2,1)S(1)}, bf16[400,512]{1,0:T(8,128)(2,1)S(1)}, u32[]{:S(2)}, u32[]{:S(2)}) collective-permute-start(bf16[400,512]{1,0:T(8,128)(2,1)S(1)} %convolution_convert_fusion), channel_id=1, source_target_pairs={{2,0},{3,1},{4,2},{5,3},{6,4},{7,5},{8,6},{9,7},{10,8},{11,9},{12,... | collective-permute-start | bytes 1228808 | tf_op jit(solution)/shard_map/ppermute | solution.py:19
